TPU v7x, 256 devices: a whole 4x4x8 slice. The times are simulated.
256 devices in a mesh: tm: 8 (over x, core), tile: 32 (over y, z).
Axes of the slice: x: 4, y: 4, z: 8, core: 2. Of those that a mesh axis runs over, the one named last changes fastest.
Arguments:
- advect_east: float32 [8, 2, 384, 1440], P('tm', None, 'tile'), may hold values from -0.15 to 0.15
- advect_north: float32 [8, 2, 384, 1440], P('tm', None, 'tile'), may hold values from -0.15 to 0.15
- diffusion: float32 [8, 2, 384, 1440], P('tm', None, 'tile'), may hold values from 0.06 to 0.22
- background_var: float32 [8, 4, 2, 384, 1440], P('tm', None, None, 'tile'), may hold values from 0.3 to 3
- obs_cell: int32 [8, 32, 1024], P('tm', 'tile'), may hold values from 0 to 138239
- obs_value: float32 [8, 32, 1024], P('tm', 'tile'), may hold values from -6 to 6
- obs_weight: float32 [8, 32, 1024], P('tm', 'tile'), may hold values from 0.5 to 2
- obs_count: int32 [8, 32, 32], P('tm', 'tile'), may hold values from 10 to 32, as said below
Outputs:
- increment: float32 [8, 4, 2, 384, 1440], P('tm', None, None, 'tile')
Inputs may be any that keep to these rules, and one draw needn't show every extreme that they name: In every sub-window one tile, drawn from the seed, gets 32 filled slots from every source device; only the first obs_count slots of a block hold observations.
All inputs are finite; a program needn't handle non-finite values.
Results may differ from a plain program's by a relative error of at most 0.00002.
Values sent between devices are 32-bit elements; how exact they have to be, the bound alone decides.
A program may use at most 128 MiB of HBM per device.

v0:
```python
import jax
import jax.numpy as jnp
from jax import lax
from jax.sharding import PartitionSpec as P

STEPS = 2
ITERS = 2


def padded(block, sides, width):
    for axis, dim in sides:
        count = lax.axis_size(axis)
        forward = [(i, i + 1) for i in range(count - 1)]
        backward = [(target, source) for source, target in forward]
        low = lax.ppermute(
            lax.slice_in_dim(block, block.shape[dim] - width, None, axis=dim), axis, forward
        )
        high = lax.ppermute(lax.slice_in_dim(block, 0, width, axis=dim), axis, backward)
        block = jnp.concatenate([low, block, high], axis=dim)
    return block


def shifted(value, axis, steps):
    count = lax.axis_size(axis)
    first, last = (max(0, -steps), min(count, count - steps))
    return lax.ppermute(value, axis, [(source, source + steps) for source in range(first, last)])


def apply_step(field, coef, adjoint):
    east_c = coef[0]
    north_c = coef[1]
    diff_c = coef[2]
    if adjoint:
        to_east = (diff_c - 0.5 * east_c) * field
        to_west = (diff_c + 0.5 * east_c) * field
        to_north = (diff_c - 0.5 * north_c) * field
        to_south = (diff_c + 0.5 * north_c) * field
        middle = (1.0 - 4.0 * diff_c[:, 1:-1]) * field[:, :, 1:-1]
        return (
            middle
            + jnp.roll(to_east[:, :, 1:-1], 1, axis=-1)
            + jnp.roll(to_west[:, :, 1:-1], -1, axis=-1)
            + to_north[:, :, :-2]
            + to_south[:, :, 2:]
        )
    inner = field[:, :, 1:-1]
    diff_in = diff_c[:, 1:-1]
    east_in = east_c[:, 1:-1]
    north_in = north_c[:, 1:-1]
    return (
        (1.0 - 4.0 * diff_in) * inner
        + (diff_in - 0.5 * east_in) * jnp.roll(inner, -1, axis=-1)
        + (diff_in + 0.5 * east_in) * jnp.roll(inner, 1, axis=-1)
        + (diff_in - 0.5 * north_in) * field[:, :, 2:]
        + (diff_in + 0.5 * north_in) * field[:, :, :-2]
    )


def advance(field, coef, adjoint):
    for repeat in range(STEPS):
        extended = padded(field, (("tile", 2),), 1)
        field = apply_step(extended, coef, adjoint)
    return field


def per_device(
    advect_east, advect_north, diffusion, background_var, obs_cell, obs_value, obs_weight, obs_count
):
    windows_count = lax.axis_size("tm")
    tiles = lax.axis_size("tile")
    coefs = jnp.stack([advect_east[0], advect_north[0], diffusion[0]])
    coef_ext = padded(coefs, (("tile", 2),), 1)
    cells = obs_cell.reshape(tiles, -1)
    slot_count = cells.shape[1]
    live = jnp.arange(slot_count, dtype=jnp.int32)[None, :] < obs_count.reshape(tiles)[:, None]
    masked = obs_weight.reshape(tiles, -1) * live.astype(jnp.float32)
    received = lax.all_to_all(
        jnp.stack([obs_value.reshape(tiles, -1), masked]),
        "tile",
        split_axis=1,
        concat_axis=1,
        tiled=True,
    )
    received_cells = lax.all_to_all(cells, "tile", split_axis=0, concat_axis=0, tiled=True)
    departures = received[0].reshape(-1)
    obs_weights = received[1].reshape(-1)
    flat_cells = received_cells.reshape(-1)
    local_var = background_var[0]
    state_shape = local_var.shape
    cell_total = state_shape[0] * state_shape[1] * state_shape[2] * state_shape[3]
    increment = jnp.zeros(state_shape, jnp.float32)
    for iteration in range(ITERS):
        if iteration == 0:
            innov = obs_weights * (0.0 - departures)
        else:
            forward_carried = advance(increment, coef_ext, False)
            for forward_window in range(windows_count - 1):
                forward_incoming = shifted(forward_carried, "tm", 1)
                forward_carried = advance(forward_incoming + increment, coef_ext, False)
            innov = obs_weights * (
                jnp.take(forward_carried.reshape(cell_total), flat_cells, axis=0) - departures
            )
        gridded = jnp.zeros((cell_total,), jnp.float32).at[flat_cells].add(innov)
        source = gridded.reshape(state_shape)
        carried = advance(source, coef_ext, True)
        for window in range(windows_count - 1):
            incoming = shifted(carried, "tm", -1)
            carried = advance(incoming + source, coef_ext, True)
        increment = increment - 0.5 * (increment + local_var * carried)
    return increment[None]


def solution(mesh):
    return jax.shard_map(
        per_device,
        mesh=mesh,
        in_specs=(
            P("tm", None, "tile", None),
            P("tm", None, "tile", None),
            P("tm", None, "tile", None),
            P("tm", None, None, "tile", None),
            P("tm", "tile", None),
            P("tm", "tile", None),
            P("tm", "tile", None),
            P("tm", "tile", None),
        ),
        out_specs=P("tm", None, None, "tile", None),
        check_vma=False,
    )
```

profile of v0, /device:TPU:1, one launch (start us, length us, event | category | flops | bytes accessed | tf_op | source)
XLA Modules:
  0.0 837.9 jit_solution(1271320414306380838)
XLA Ops:
  9.6 13.0 %all-to-all-start = ((s32[32,1,32]{2,1,0:T(1,128)}), s32[32,1,32]{2,1,0:T(1,128)S(1)}, u32[]{:S(2)}, u32[]{:S(2)}) async-start(s32[32,1,32]{2,1,0:T(1,128)} %all_to_all.9), calls=%async_computation | async-start | bytes 32768 | tf_op jit(solution)/shard_map/all_to_all | solution.py:84
  36.7 7.9 all-to-all-done.1
  44.9 6.1 scatter_custom_fusion
  68.8 8.0 collective-permute-start.6
  76.8 8.6 %collective-permute-done.6 = f32[4,2,12,1440]{3,0,2,1:T(4,128)S(1)} collective-permute-done((f32[4,2,12,1440]{3,0,2,1:T(4,128)S(1)}, f32[4,2,12,1440]{3,0,2,1:T(4,128)S(1)}, u32[]{:S(2)}, u32[]{:S(2)}) %collective-permute-start.6) | collective-permute-done | bytes 552992 | tf_op jit(solution)/shard_map/ppermute | solution.py:26
  104.2 9.8 %collective-permute-done.11 = f32[4,2,12,1440]{3,0,2,1:T(4,128)S(1)} collective-permute-done((f32[4,2,12,1440]{3,0,2,1:T(4,128)S(1)}, f32[4,2,12,1440]{3,0,2,1:T(4,128)S(1)}, u32[]{:S(2)}, u32[]{:S(2)}) %collective-permute-start.11) | collective-permute-done | bytes 552992 | tf_op jit(solution)/shard_map/ppermute | solution.py:26
  139.2 9.8 %collective-permute-done.16 = f32[4,2,12,1440]{3,0,2,1:T(4,128)S(1)} collective-permute-done((f32[4,2,12,1440]{3,0,2,1:T(4,128)S(1)}, f32[4,2,12,1440]{3,0,2,1:T(4,128)S(1)}, u32[]{:S(2)}, u32[]{:S(2)}) %collective-permute-start.16) | collective-permute-done | bytes 552992 | tf_op jit(solution)/shard_map/ppermute | solution.py:26
  174.1 9.6 %collective-permute-done.21 = f32[4,2,12,1440]{3,0,2,1:T(4,128)S(1)} collective-permute-done((f32[4,2,12,1440]{3,0,2,1:T(4,128)S(1)}, f32[4,2,12,1440]{3,0,2,1:T(4,128)S(1)}, u32[]{:S(2)}, u32[]{:S(2)}) %collective-permute-start.21) | collective-permute-done | bytes 552992 | tf_op jit(solution)/shard_map/ppermute | solution.py:26
  209.4 10.5 %collective-permute-done.26 = f32[4,2,12,1440]{3,0,2,1:T(4,128)S(1)} collective-permute-done((f32[4,2,12,1440]{3,0,2,1:T(4,128)S(1)}, f32[4,2,12,1440]{3,0,2,1:T(4,128)S(1)}, u32[]{:S(2)}, u32[]{:S(2)}) %collective-permute-start.26) | collective-permute-done | bytes 552992 | tf_op jit(solution)/shard_map/ppermute | solution.py:26
  242.6 10.1 %collective-permute-done.31 = f32[4,2,12,1440]{3,0,2,1:T(4,128)S(1)} collective-permute-done((f32[4,2,12,1440]{3,0,2,1:T(4,128)S(1)}, f32[4,2,12,1440]{3,0,2,1:T(4,128)S(1)}, u32[]{:S(2)}, u32[]{:S(2)}) %collective-permute-start.31) | collective-permute-done | bytes 552992 | tf_op jit(solution)/shard_map/ppermute | solution.py:26
  275.7 10.0 %collective-permute-done.36 = f32[4,2,12,1440]{3,0,2,1:T(4,128)S(1)} collective-permute-done((f32[4,2,12,1440]{3,0,2,1:T(4,128)S(1)}, f32[4,2,12,1440]{3,0,2,1:T(4,128)S(1)}, u32[]{:S(2)}, u32[]{:S(2)}) %collective-permute-start.36) | collective-permute-done | bytes 552992 | tf_op jit(solution)/shard_map/ppermute | solution.py:26
  322.9 6.9 collective-permute-start.45
  329.8 6.8 collective-permute-done.45
  353.7 5.8 collective-permute-start.50
  359.5 6.8 collective-permute-done.50
  385.4 6.1 collective-permute-start.55
  391.5 6.8 collective-permute-done.55
  400.2 5.8 collective-permute-start.57
  417.3 6.1 collective-permute-start.60
  423.5 6.8 collective-permute-done.60
  449.3 6.1 collective-permute-start.65
  455.4 6.8 collective-permute-done.65
  464.1 6.0 collective-permute-start.67
  481.3 6.1 collective-permute-start.70
  487.4 6.8 collective-permute-done.70
  505.3 5.8 collective-permute-start.74
  513.2 6.1 collective-permute-start.75
  519.4 6.7 collective-permute-done.75
  529.1 5.8 collective-permute-start.77
  538.3 6.2 collective-permute-start.79
  546.8 6.2 gather_fusion
  552.9 6.1 scatter_custom_fusion.1
  559.6 6.1 collective-permute-start.80
  566.9 6.2 collective-permute-done.81
  574.5 6.1 collective-permute-start.82
  582.1 6.0 collective-permute-done.83
  591.7 14.1 %collective-permute-done.84 = f32[4,2,12,1440]{3,0,2,1:T(4,128)S(1)} collective-permute-done((f32[4,2,12,1440]{3,0,2,1:T(4,128)S(1)}, f32[4,2,12,1440]{3,0,2,1:T(4,128)S(1)}, u32[]{:S(2)}, u32[]{:S(2)}) %collective-permute-start.84) | collective-permute-done | bytes 552992 | tf_op jit(solution)/shard_map/ppermute | solution.py:26
  606.2 6.1 collective-permute-start.85
  613.6 6.2 collective-permute-done.86
  621.2 6.1 collective-permute-start.87
  628.6 6.2 collective-permute-done.88
  638.4 9.7 %collective-permute-done.89 = f32[4,2,12,1440]{3,0,2,1:T(4,128)S(1)} collective-permute-done((f32[4,2,12,1440]{3,0,2,1:T(4,128)S(1)}, f32[4,2,12,1440]{3,0,2,1:T(4,128)S(1)}, u32[]{:S(2)}, u32[]{:S(2)}) %collective-permute-start.89) | collective-permute-done | bytes 552992 | tf_op jit(solution)/shard_map/ppermute | solution.py:26
  648.4 6.0 collective-permute-start.90
  674.3 10.1 %collective-permute-done.94 = f32[4,2,12,1440]{3,0,2,1:T(4,128)S(1)} collective-permute-done((f32[4,2,12,1440]{3,0,2,1:T(4,128)S(1)}, f32[4,2,12,1440]{3,0,2,1:T(4,128)S(1)}, u32[]{:S(2)}, u32[]{:S(2)}) %collective-permute-start.94) | collective-permute-done | bytes 552992 | tf_op jit(solution)/shard_map/ppermute | solution.py:26
  707.1 10.3 %collective-permute-done.99 = f32[4,2,12,1440]{3,0,2,1:T(4,128)S(1)} collective-permute-done((f32[4,2,12,1440]{3,0,2,1:T(4,128)S(1)}, f32[4,2,12,1440]{3,0,2,1:T(4,128)S(1)}, u32[]{:S(2)}, u32[]{:S(2)}) %collective-permute-start.99) | collective-permute-done | bytes 552992 | tf_op jit(solution)/shard_map/ppermute | solution.py:26
  739.8 10.3 %collective-permute-done.104 = f32[4,2,12,1440]{3,0,2,1:T(4,128)S(1)} collective-permute-done((f32[4,2,12,1440]{3,0,2,1:T(4,128)S(1)}, f32[4,2,12,1440]{3,0,2,1:T(4,128)S(1)}, u32[]{:S(2)}, u32[]{:S(2)}) %collective-permute-start.104) | collective-permute-done | bytes 552992 | tf_op jit(solution)/shard_map/ppermute | solution.py:26
  772.4 10.3 %collective-permute-done.109 = f32[4,2,12,1440]{3,0,2,1:T(4,128)S(1)} collective-permute-done((f32[4,2,12,1440]{3,0,2,1:T(4,128)S(1)}, f32[4,2,12,1440]{3,0,2,1:T(4,128)S(1)}, u32[]{:S(2)}, u32[]{:S(2)}) %collective-permute-start.109) | collective-permute-done | bytes 552992 | tf_op jit(solution)/shard_map/ppermute | solution.py:26
  805.1 10.3 %collective-permute-done.114 = f32[4,2,12,1440]{3,0,2,1:T(4,128)S(1)} collective-permute-done((f32[4,2,12,1440]{3,0,2,1:T(4,128)S(1)}, f32[4,2,12,1440]{3,0,2,1:T(4,128)S(1)}, u32[]{:S(2)}, u32[]{:S(2)}) %collective-permute-start.114) | collective-permute-done | bytes 552992 | tf_op jit(solution)/shard_map/ppermute | solution.py:26
  (617 shorter events, 467.9 us)
Async XLA Ops:
  1.9 53.2 %collective-permute-start = (f32[3,2,1,1440]{3,1,2,0:T(2,128)S(1)}, f32[3,2,1,1440]{3,1,2,0:T(2,128)S(1)}, u32[]{:S(2)}, u32[]{:S(2)}) collective-permute-start(f32[3,2,1,1440]{3,1,2,0:T(2,128)S(1)} %get-tuple-element.238), channel_id=1, source_target_pairs={{0,1},{1,2},{2,3},{3,4},{4,5},{5,6},{6,7},{7,8},{8,9},{9,10},{10,1... | collective-permute-start | bytes 103688 | tf_op jit(solution)/shard_map/ppermute | solution.py:15
  6.3 48.9 %collective-permute-start.1 = (f32[3,2,1,1440]{3,1,2,0:T(2,128)S(1)}, f32[3,2,1,1440]{3,1,2,0:T(2,128)S(1)}, u32[]{:S(2)}, u32[]{:S(2)}) collective-permute-start(f32[3,2,1,1440]{3,1,2,0:T(2,128)S(1)} %get-tuple-element.239), channel_id=1, source_target_pairs={{1,0},{2,1},{3,2},{4,3},{5,4},{6,5},{7,6},{8,7},{9,8},{10,9},{11,1... | collective-permute-start | bytes 103688 | tf_op jit(solution)/shard_map/ppermute | solution.py:18
  9.6 21.7 %all-to-all-start = ((s32[32,1,32]{2,1,0:T(1,128)}), s32[32,1,32]{2,1,0:T(1,128)S(1)}, u32[]{:S(2)}, u32[]{:S(2)}) async-start(s32[32,1,32]{2,1,0:T(1,128)} %all_to_all.9), calls=%async_computation | async-start | bytes 32768 | tf_op jit(solution)/shard_map/all_to_all | solution.py:84
  31.3 13.4 %all-to-all-start.1 = ((f32[2,32,32]{2,0,1:T(2,128)}), f32[2,32,32]{2,0,1:T(2,128)S(1)}, u32[]{:S(2)}, u32[]{:S(2)}) async-start(f32[2,32,32]{2,0,1:T(2,128)} %pad_maximum_fusion.65), calls=%async_computation.1 | async-start | bytes 65536 | tf_op jit(solution)/shard_map/all_to_all | solution.py:77
  68.8 16.6 %collective-permute-start.6 = (f32[4,2,12,1440]{3,0,2,1:T(4,128)S(1)}, f32[4,2,12,1440]{3,0,2,1:T(4,128)S(1)}, u32[]{:S(2)}, u32[]{:S(2)}) collective-permute-start(f32[4,2,12,1440]{3,0,2,1:T(4,128)S(1)} %copy.26), channel_id=1, source_target_pairs={{32,0},{64,32},{96,64},{128,96},{160,128},{192,160},{224,192},{33,... | collective-permute-start | bytes 1658888 | tf_op jit(solution)/shard_map/ppermute | solution.py:26
  102.2 11.8 %collective-permute-start.11 = (f32[4,2,12,1440]{3,0,2,1:T(4,128)S(1)}, f32[4,2,12,1440]{3,0,2,1:T(4,128)S(1)}, u32[]{:S(2)}, u32[]{:S(2)}) collective-permute-start(f32[4,2,12,1440]{3,0,2,1:T(4,128)S(1)} %copy.28), channel_id=1, source_target_pairs={{32,0},{64,32},{96,64},{128,96},{160,128},{192,160},{224,192},{33,... | collective-permute-start | bytes 1658888 | tf_op jit(solution)/shard_map/ppermute | solution.py:26
  137.3 11.8 %collective-permute-start.16 = (f32[4,2,12,1440]{3,0,2,1:T(4,128)S(1)}, f32[4,2,12,1440]{3,0,2,1:T(4,128)S(1)}, u32[]{:S(2)}, u32[]{:S(2)}) collective-permute-start(f32[4,2,12,1440]{3,0,2,1:T(4,128)S(1)} %copy.30), channel_id=1, source_target_pairs={{32,0},{64,32},{96,64},{128,96},{160,128},{192,160},{224,192},{33,... | collective-permute-start | bytes 1658888 | tf_op jit(solution)/shard_map/ppermute | solution.py:26
  172.1 11.6 %collective-permute-start.21 = (f32[4,2,12,1440]{3,0,2,1:T(4,128)S(1)}, f32[4,2,12,1440]{3,0,2,1:T(4,128)S(1)}, u32[]{:S(2)}, u32[]{:S(2)}) collective-permute-start(f32[4,2,12,1440]{3,0,2,1:T(4,128)S(1)} %copy.32), channel_id=1, source_target_pairs={{32,0},{64,32},{96,64},{128,96},{160,128},{192,160},{224,192},{33,... | collective-permute-start | bytes 1658888 | tf_op jit(solution)/shard_map/ppermute | solution.py:26
  184.0 7.0 collective-permute-start.22
  207.5 12.4 %collective-permute-start.26 = (f32[4,2,12,1440]{3,0,2,1:T(4,128)S(1)}, f32[4,2,12,1440]{3,0,2,1:T(4,128)S(1)}, u32[]{:S(2)}, u32[]{:S(2)}) collective-permute-start(f32[4,2,12,1440]{3,0,2,1:T(4,128)S(1)} %copy.34), channel_id=1, source_target_pairs={{32,0},{64,32},{96,64},{128,96},{160,128},{192,160},{224,192},{33,... | collective-permute-start | bytes 1658888 | tf_op jit(solution)/shard_map/ppermute | solution.py:26
  240.7 12.0 %collective-permute-start.31 = (f32[4,2,12,1440]{3,0,2,1:T(4,128)S(1)}, f32[4,2,12,1440]{3,0,2,1:T(4,128)S(1)}, u32[]{:S(2)}, u32[]{:S(2)}) collective-permute-start(f32[4,2,12,1440]{3,0,2,1:T(4,128)S(1)} %copy.36), channel_id=1, source_target_pairs={{32,0},{64,32},{96,64},{128,96},{160,128},{192,160},{224,192},{33,... | collective-permute-start | bytes 1658888 | tf_op jit(solution)/shard_map/ppermute | solution.py:26
  273.8 11.9 %collective-permute-start.36 = (f32[4,2,12,1440]{3,0,2,1:T(4,128)S(1)}, f32[4,2,12,1440]{3,0,2,1:T(4,128)S(1)}, u32[]{:S(2)}, u32[]{:S(2)}) collective-permute-start(f32[4,2,12,1440]{3,0,2,1:T(4,128)S(1)} %copy.38), channel_id=1, source_target_pairs={{32,0},{64,32},{96,64},{128,96},{160,128},{192,160},{224,192},{33,... | collective-permute-start | bytes 1658888 | tf_op jit(solution)/shard_map/ppermute | solution.py:26
  322.9 13.7 %collective-permute-start.45 = (f32[4,2,12,1440]{3,0,2,1:T(4,128)S(1)}, f32[4,2,12,1440]{3,0,2,1:T(4,128)S(1)}, u32[]{:S(2)}, u32[]{:S(2)}) collective-permute-start(f32[4,2,12,1440]{3,0,2,1:T(4,128)S(1)} %copy.44), channel_id=1, source_target_pairs={{0,32},{32,64},{64,96},{96,128},{128,160},{160,192},{192,224},{1,3... | collective-permute-start | bytes 1658888 | tf_op jit(solution)/shard_map/ppermute | solution.py:26
  353.7 12.6 %collective-permute-start.50 = (f32[4,2,12,1440]{3,0,2,1:T(4,128)S(1)}, f32[4,2,12,1440]{3,0,2,1:T(4,128)S(1)}, u32[]{:S(2)}, u32[]{:S(2)}) collective-permute-start(f32[4,2,12,1440]{3,0,2,1:T(4,128)S(1)} %copy.46), channel_id=1, source_target_pairs={{0,32},{32,64},{64,96},{96,128},{128,160},{160,192},{192,224},{1,3... | collective-permute-start | bytes 1658888 | tf_op jit(solution)/shard_map/ppermute | solution.py:26
  366.9 7.2 collective-permute-start.51
  376.1 7.2 collective-permute-start.53
  385.4 12.9 %collective-permute-start.55 = (f32[4,2,12,1440]{3,0,2,1:T(4,128)S(1)}, f32[4,2,12,1440]{3,0,2,1:T(4,128)S(1)}, u32[]{:S(2)}, u32[]{:S(2)}) collective-permute-start(f32[4,2,12,1440]{3,0,2,1:T(4,128)S(1)} %copy.48), channel_id=1, source_target_pairs={{0,32},{32,64},{64,96},{96,128},{128,160},{160,192},{192,224},{1,3... | collective-permute-start | bytes 1658888 | tf_op jit(solution)/shard_map/ppermute | solution.py:26
  398.9 7.2 collective-permute-start.56
  408.1 7.2 collective-permute-start.58
  417.3 12.9 %collective-permute-start.60 = (f32[4,2,12,1440]{3,0,2,1:T(4,128)S(1)}, f32[4,2,12,1440]{3,0,2,1:T(4,128)S(1)}, u32[]{:S(2)}, u32[]{:S(2)}) collective-permute-start(f32[4,2,12,1440]{3,0,2,1:T(4,128)S(1)} %copy.50), channel_id=1, source_target_pairs={{0,32},{32,64},{64,96},{96,128},{128,160},{160,192},{192,224},{1,3... | collective-permute-start | bytes 1658888 | tf_op jit(solution)/shard_map/ppermute | solution.py:26
  430.9 7.2 collective-permute-start.61
  440.1 7.2 collective-permute-start.63
  449.3 12.9 %collective-permute-start.65 = (f32[4,2,12,1440]{3,0,2,1:T(4,128)S(1)}, f32[4,2,12,1440]{3,0,2,1:T(4,128)S(1)}, u32[]{:S(2)}, u32[]{:S(2)}) collective-permute-start(f32[4,2,12,1440]{3,0,2,1:T(4,128)S(1)} %copy.52), channel_id=1, source_target_pairs={{0,32},{32,64},{64,96},{96,128},{128,160},{160,192},{192,224},{1,3... | collective-permute-start | bytes 1658888 | tf_op jit(solution)/shard_map/ppermute | solution.py:26
  462.8 7.4 collective-permute-start.66
  472.0 7.2 collective-permute-start.68
  481.3 12.9 %collective-permute-start.70 = (f32[4,2,12,1440]{3,0,2,1:T(4,128)S(1)}, f32[4,2,12,1440]{3,0,2,1:T(4,128)S(1)}, u32[]{:S(2)}, u32[]{:S(2)}) collective-permute-start(f32[4,2,12,1440]{3,0,2,1:T(4,128)S(1)} %copy.54), channel_id=1, source_target_pairs={{0,32},{32,64},{64,96},{96,128},{128,160},{160,192},{192,224},{1,3... | collective-permute-start | bytes 1658888 | tf_op jit(solution)/shard_map/ppermute | solution.py:26
  494.8 7.2 collective-permute-start.71
  504.0 7.2 collective-permute-start.73
  513.2 12.9 %collective-permute-start.75 = (f32[4,2,12,1440]{3,0,2,1:T(4,128)S(1)}, f32[4,2,12,1440]{3,0,2,1:T(4,128)}, u32[]{:S(2)}, u32[]{:S(2)}) collective-permute-start(f32[4,2,12,1440]{3,0,2,1:T(4,128)S(1)} %copy.56), channel_id=1, source_target_pairs={{0,32},{32,64},{64,96},{96,128},{128,160},{160,192},{192,224},{1,3... | collective-permute-start | bytes 1658888 | tf_op jit(solution)/shard_map/ppermute | solution.py:26
  527.8 7.2 collective-permute-start.76
  537.0 7.6 collective-permute-start.78
  538.3 7.4 collective-permute-start.79
  559.6 7.4 collective-permute-start.80
  565.6 7.6 collective-permute-start.81
  574.5 7.6 collective-permute-start.82
  580.6 7.6 collective-permute-start.83
  589.8 16.1 %collective-permute-start.84 = (f32[4,2,12,1440]{3,0,2,1:T(4,128)S(1)}, f32[4,2,12,1440]{3,0,2,1:T(4,128)S(1)}, u32[]{:S(2)}, u32[]{:S(2)}) collective-permute-start(f32[4,2,12,1440]{3,0,2,1:T(4,128)S(1)} %copy.58), channel_id=1, source_target_pairs={{32,0},{64,32},{96,64},{128,96},{160,128},{192,160},{224,192},{33,... | collective-permute-start | bytes 1658888 | tf_op jit(solution)/shard_map/ppermute | solution.py:26
  606.2 7.4 collective-permute-start.85
  612.3 7.6 collective-permute-start.86
  621.2 7.4 collective-permute-start.87
  627.2 7.6 collective-permute-start.88
  636.4 11.6 %collective-permute-start.89 = (f32[4,2,12,1440]{3,0,2,1:T(4,128)S(1)}, f32[4,2,12,1440]{3,0,2,1:T(4,128)S(1)}, u32[]{:S(2)}, u32[]{:S(2)}) collective-permute-start(f32[4,2,12,1440]{3,0,2,1:T(4,128)S(1)} %copy.60), channel_id=1, source_target_pairs={{32,0},{64,32},{96,64},{128,96},{160,128},{192,160},{224,192},{33,... | collective-permute-start | bytes 1658888 | tf_op jit(solution)/shard_map/ppermute | solution.py:26
  648.4 7.3 collective-permute-start.90
  672.3 12.0 %collective-permute-start.94 = (f32[4,2,12,1440]{3,0,2,1:T(4,128)S(1)}, f32[4,2,12,1440]{3,0,2,1:T(4,128)S(1)}, u32[]{:S(2)}, u32[]{:S(2)}) collective-permute-start(f32[4,2,12,1440]{3,0,2,1:T(4,128)S(1)} %copy.62), channel_id=1, source_target_pairs={{32,0},{64,32},{96,64},{128,96},{160,128},{192,160},{224,192},{33,... | collective-permute-start | bytes 1658888 | tf_op jit(solution)/shard_map/ppermute | solution.py:26
  705.2 12.2 %collective-permute-start.99 = (f32[4,2,12,1440]{3,0,2,1:T(4,128)S(1)}, f32[4,2,12,1440]{3,0,2,1:T(4,128)S(1)}, u32[]{:S(2)}, u32[]{:S(2)}) collective-permute-start(f32[4,2,12,1440]{3,0,2,1:T(4,128)S(1)} %copy.64), channel_id=1, source_target_pairs={{32,0},{64,32},{96,64},{128,96},{160,128},{192,160},{224,192},{33,... | collective-permute-start | bytes 1658888 | tf_op jit(solution)/shard_map/ppermute | solution.py:26
  737.8 12.2 %collective-permute-start.104 = (f32[4,2,12,1440]{3,0,2,1:T(4,128)S(1)}, f32[4,2,12,1440]{3,0,2,1:T(4,128)S(1)}, u32[]{:S(2)}, u32[]{:S(2)}) collective-permute-start(f32[4,2,12,1440]{3,0,2,1:T(4,128)S(1)} %copy.66), channel_id=1, source_target_pairs={{32,0},{64,32},{96,64},{128,96},{160,128},{192,160},{224,192},{33,... | collective-permute-start | bytes 1658888 | tf_op jit(solution)/shard_map/ppermute | solution.py:26
  770.5 12.2 %collective-permute-start.109 = (f32[4,2,12,1440]{3,0,2,1:T(4,128)S(1)}, f32[4,2,12,1440]{3,0,2,1:T(4,128)S(1)}, u32[]{:S(2)}, u32[]{:S(2)}) collective-permute-start(f32[4,2,12,1440]{3,0,2,1:T(4,128)S(1)} %copy.68), channel_id=1, source_target_pairs={{32,0},{64,32},{96,64},{128,96},{160,128},{192,160},{224,192},{33,... | collective-permute-start | bytes 1658888 | tf_op jit(solution)/shard_map/ppermute | solution.py:26
  803.2 12.2 %collective-permute-start.114 = (f32[4,2,12,1440]{3,0,2,1:T(4,128)S(1)}, f32[4,2,12,1440]{3,0,2,1:T(4,128)S(1)}, u32[]{:S(2)}, u32[]{:S(2)}) collective-permute-start(f32[4,2,12,1440]{3,0,2,1:T(4,128)S(1)} %copy.70), channel_id=1, source_target_pairs={{32,0},{64,32},{96,64},{128,96},{160,128},{192,160},{224,192},{33,... | collective-permute-start | bytes 1658888 | tf_op jit(solution)/shard_map/ppermute | solution.py:26
  (81 other events, 422.8 us)
where the time goes:
time: 853 us; the launch traced here: 838 us
  starting transfers between devices  384 us (45%)
  waiting for transfers between devices  346 us (41%)
  other arithmetic  56.7 us (7%)
  local copies, waits for them, and re-layouts  47.9 us (6%)
    ppermute x49, starting transfers between devices, padded(): lax.ppermute(lax.slice_in_dim(block, block.shape[dim] - width, None, axis...  226 us
    ppermute x21, waiting for transfers between devices, shifted(): lax.ppermute(value, axis, [(source, source + steps) for source in range(f...  191 us
    ppermute x49, waiting for transfers between devices, padded(): lax.ppermute(lax.slice_in_dim(block, 0, width, axis=dim), axis, backward)  123 us
    ppermute x21, starting transfers between devices, shifted(): lax.ppermute(value, axis, [(source, source + steps) for source in range(f...  76.1 us
    ppermute x49, starting transfers between devices, padded(): lax.ppermute(lax.slice_in_dim(block, 0, width, axis=dim), axis, backward)  64.3 us
    ppermute x49, waiting for transfers between devices, padded(): lax.ppermute(lax.slice_in_dim(block, block.shape[dim] - width, None, axis...  18.5 us
  transfers between devices with their start and end apart: 121, of which 71 were waited for; matrix products, arithmetic and copies ran while one was open for 2% of the time, Pallas kernels for 0%

commit v1 on v0

v1 whole, which is shorter than its diff:
```python
import functools

import jax
import jax.numpy as jnp
from jax import lax
from jax.experimental import pallas as pl
from jax.experimental.pallas import tpu as pltpu
from jax.sharding import PartitionSpec as P

MESH = pl.DeviceIdType.MESH
F32 = jnp.float32
BF16 = jnp.bfloat16
LON = 1440
LAT = 12
CAP = 32
FIELDS = 8
LANES = 256
GROUP = 2
HALO = 2 * GROUP
ROWS = LAT + 2 * HALO


def split3(value):
    high = value.astype(BF16).astype(F32)
    rest = value - high
    middle = rest.astype(BF16).astype(F32)
    return high, middle, rest - middle


def kernel(
    windows,
    tiles,
    coef_in,
    bv_in,
    obs_in,
    out_ref,
    obs1,
    obsall,
    craw,
    crawn,
    craws,
    der,
    bvr,
    hot,
    src,
    srcn,
    srcs,
    inc,
    incn,
    incs,
    states,
    final,
    carry,
    carryn,
    carrys,
    work,
    innov,
    innovl,
    innovr,
    obs_s,
    obs_r,
    ob2_s,
    ob2_r,
    c_s,
    c_r,
    ch_s,
    ch_r,
    bv_s,
    bv_r,
    src_s,
    src_r,
    inc_s,
    inc_r,
    car_s,
    car_r,
    inn_s,
    inn_r,
    out_s,
    out_r,
):
    m = lax.axis_index("tm")
    t = lax.axis_index("tile")
    chunk = LON // windows
    margin = (LANES - chunk) // 2
    groups = windows // GROUP
    slots = obsall.shape[-1]
    cells = LAT * FIELDS
    up = lax.rem(t + 1, tiles)
    down = lax.rem(t + tiles - 1, tiles)
    left = lax.rem(m + windows - 1, windows)
    right = lax.rem(m + 1, windows)
    edge_low = jnp.where(t == 0, 0.0, 1.0).astype(F32)
    edge_high = jnp.where(t == tiles - 1, 0.0, 1.0).astype(F32)

    barrier = pltpu.get_barrier_semaphore()

    def greet_tile(d, token):
        pl.semaphore_signal(
            barrier, inc=1, device_id=(m, lax.rem(t + d, tiles)), device_id_type=MESH
        )
        return token

    def greet_tm(d, token):
        pl.semaphore_signal(
            barrier, inc=1, device_id=(lax.rem(m + d, windows), t), device_id_type=MESH
        )
        return token

    lax.fori_loop(1, tiles, greet_tile, 0)
    lax.fori_loop(1, windows, greet_tm, 0)
    pl.semaphore_wait(barrier, tiles - 1 + windows - 1)

    def remote(source, target, send, recv, where):
        return pltpu.make_async_remote_copy(
            src_ref=source,
            dst_ref=target,
            send_sem=send,
            recv_sem=recv,
            device_id=where,
            device_id_type=MESH,
        )

    def obs_copy(d):
        peer = lax.rem(t + d, tiles)
        return remote(obs_in.at[peer], obs1.at[t], obs_s.at[d], obs_r.at[d], (m, peer))

    def obs_start(d, token):
        obs_copy(d).start()
        return token

    lax.fori_loop(1, tiles, obs_start, 0)

    coef_own = pltpu.make_async_copy(coef_in.at[m], craw.at[m], c_s.at[0])
    coef_own.start()
    bv_own = pltpu.make_async_copy(bv_in.at[m], bvr.at[m], bv_s.at[0])

    def coef_copy(d):
        peer = lax.rem(m + d, windows)
        return remote(coef_in.at[peer], craw.at[m], c_s.at[d], c_r.at[m], (peer, t))

    def bv_copy(d):
        peer = lax.rem(m + d, windows)
        return remote(bv_in.at[peer], bvr.at[m], bv_s.at[d], bv_r.at[m], (peer, t))

    def coef_start(d, token):
        coef_copy(d).start()
        return token

    lax.fori_loop(1, windows, coef_start, 0)

    for ref in (carry, carryn, carrys):
        for sweep in range(3):
            ref[sweep * groups] = jnp.zeros(ref.shape[1:], F32)

    obs1[t] = obs_in[t]

    def obs_wait(d, token):
        obs_copy(d).wait_recv()
        return token

    lax.fori_loop(1, tiles, obs_wait, 0)
    for j in range(tiles // 4):
        obsall[m, :, j * 128 : (j + 1) * 128] = (
            obs1[4 * j] + obs1[4 * j + 1] + obs1[4 * j + 2] + obs1[4 * j + 3]
        )

    def ob2_copy(d):
        peer = lax.rem(m + d, windows)
        return remote(obsall.at[m], obsall.at[m], ob2_s.at[d], ob2_r.at[m], (peer, t))

    def ob2_start(d, token):
        ob2_copy(d).start()
        return token

    lax.fori_loop(1, windows, ob2_start, 0)
    bv_own.start()

    def bv_start(d, token):
        bv_copy(d).start()
        return token

    lax.fori_loop(1, windows, bv_start, 0)

    def from_peer(ref, sem, k, own):
        @pl.when(k != m)
        def _():
            remote(ref.at[k], ref.at[k], sem.at[k], sem.at[k], (k, t)).wait_recv()

        if own is not None:

            @pl.when(k == m)
            def _():
                own.wait()

    edge_tiles = HALO * 6 // 8

    def coef_low(k):
        return remote(
            craw.at[k, 0:edge_tiles], craws.at[k], ch_s.at[0, k], ch_r.at[0, k], (m, down)
        )

    def coef_high(k):
        return remote(
            craw.at[k, 9 - edge_tiles : 9], crawn.at[k], ch_s.at[1, k], ch_r.at[1, k], (m, up)
        )

    def coef_forward(i, token):
        k = windows - 1 - i
        from_peer(craw, c_r, k, coef_own)
        coef_low(k).start()
        coef_high(k).start()
        return token

    lower = lax.broadcasted_iota(jnp.int32, (FIELDS, LANES), 0) < FIELDS // 2

    def expand(k):
        coef_low(k).wait_recv()
        coef_high(k).wait_recv()
        for r in range(ROWS):
            if r < HALO:
                ref, row, edge = crawn, r, edge_low
            elif r < HALO + LAT:
                ref, row, edge = craw, r - HALO, None
            else:
                ref, row, edge = craws, r - HALO - LAT, edge_high
            picked = []
            for c in range(3):
                q = (row * 3 + c) * 2
                one = ref[k, q // 8, q % 8 : q % 8 + 1, :]
                two = ref[k, q // 8, q % 8 + 1 : q % 8 + 2, :]
                picked.append(
                    jnp.where(
                        lower,
                        jnp.broadcast_to(one, (FIELDS, LANES)),
                        jnp.broadcast_to(two, (FIELDS, LANES)),
                    )
                )
            half_east, half_north, kap = 0.5 * picked[0], 0.5 * picked[1], picked[2]
            made = (
                1.0 - 4.0 * kap,
                kap - half_east,
                kap + half_east,
                kap - half_north,
                kap + half_north,
            )
            for c in range(5):
                der[k, c, r] = made[c] if edge is None else made[c] * edge

    base = m * chunk - margin

    def lane_of(k):
        rel = obsall[k, 1:2, :].astype(jnp.int32) - base
        rel = jnp.where(rel >= LON, rel - LON, rel)
        return jnp.where(rel < 0, rel + LON, rel)

    def make_hot(k):
        rel = lane_of(k)
        lanes = lax.broadcasted_iota(jnp.int32, (LANES, slots), 0)
        hot[k] = jnp.where(lanes == rel, 1.0, 0.0).astype(BF16)

    def row_mask(k):
        rows = lax.broadcasted_iota(jnp.int32, (cells, slots), 0)
        return rows == obsall[k, 0:1, :].astype(jnp.int32)

    def scatter(it, k, value):
        mask = row_mask(k)
        parts = [jnp.where(mask, part, 0.0).astype(BF16) for part in split3(value)]
        sums = lax.dot_general(
            jnp.concatenate(parts, axis=0),
            hot[k],
            (((1,), (1,)), ((), ())),
            preferred_element_type=F32,
        )
        total = sums[2 * cells :] + sums[cells : 2 * cells] + sums[:cells]
        src[it, k] = total.reshape(LAT, FIELDS, LANES)

    def src_low(it, k):
        return remote(
            src.at[it, pl.ds(k, GROUP), 0:HALO],
            srcs.at[it, pl.ds(k, GROUP)],
            src_s.at[it, 0, k // GROUP],
            src_r.at[it, 0, k // GROUP],
            (m, down),
        )

    def src_high(it, k):
        return remote(
            src.at[it, pl.ds(k, GROUP), LAT - HALO : LAT],
            srcn.at[it, pl.ds(k, GROUP)],
            src_s.at[it, 1, k // GROUP],
            src_r.at[it, 1, k // GROUP],
            (m, up),
        )

    def inc_low(k):
        return remote(
            inc.at[pl.ds(k, GROUP), 0:HALO],
            incs.at[pl.ds(k, GROUP)],
            inc_s.at[0, k // GROUP],
            inc_r.at[0, k // GROUP],
            (m, down),
        )

    def inc_high(k):
        return remote(
            inc.at[pl.ds(k, GROUP), LAT - HALO : LAT],
            incn.at[pl.ds(k, GROUP)],
            inc_s.at[1, k // GROUP],
            inc_r.at[1, k // GROUP],
            (m, up),
        )

    def carry_low(e):
        return remote(
            carry.at[e, 0:HALO], carrys.at[e], car_s.at[0, e], car_r.at[0, e], (m, down)
        )

    def carry_high(e):
        return remote(
            carry.at[e, LAT - HALO : LAT], carryn.at[e], car_s.at[1, e], car_r.at[1, e], (m, up)
        )

    def innov_left(k):
        return remote(
            innov.at[pl.ds(k, GROUP)],
            innovr.at[pl.ds(k, GROUP)],
            inn_s.at[0, k // GROUP],
            inn_r.at[0, k // GROUP],
            (left, t),
        )

    def innov_right(k):
        return remote(
            innov.at[pl.ds(k, GROUP)],
            innovl.at[pl.ds(k, GROUP)],
            inn_s.at[1, k // GROUP],
            inn_r.at[1, k // GROUP],
            (right, t),
        )

    def three(north, own, south, index, r):
        if r < HALO:
            return north[index + (r,)]
        if r < HALO + LAT:
            return own[index + (r - HALO,)]
        return south[index + (r - HALO - LAT,)]

    def adjoint_step(load, store, k, low, high):
        to_next = None
        held = None
        for r in range(low, high):
            x = load(r)
            south = der[k, 4, r] * x
            if held is not None and r - 1 >= low + 1:
                store(r - 1, held + south)
            if r < high - 1 and r > low:
                held = (
                    der[k, 0, r] * x
                    + pltpu.roll(der[k, 1, r] * x, 1, 1)
                    + pltpu.roll(der[k, 2, r] * x, LANES - 1, 1)
                    + to_next
                )
            to_next = der[k, 3, r] * x

    def forward_step(load, store, k, low, high):
        before, here = load(low), load(low + 1)
        for r in range(low + 1, high - 1):
            after = load(r + 1)
            store(
                r,
                der[k, 0, r] * here
                + der[k, 1, r] * pltpu.roll(here, LANES - 1, 1)
                + der[k, 2, r] * pltpu.roll(here, 1, 1)
                + der[k, 3, r] * after
                + der[k, 4, r] * before,
            )
            before, here = here, after

    def keep(slot):
        def store(r, value):
            work[slot, r] = value

        return store

    def wait_carry(i, e):
        @pl.when(i > 0)
        def _():
            carry_low(e).wait_recv()
            carry_high(e).wait_recv()

    def send_carry(i, e):
        @pl.when(i < groups - 1)
        def _():
            carry_low(e).start()
            carry_high(e).start()

    def adjoint_group(it, i, done):
        e = 2 * it * groups + i
        top = windows - 1 - GROUP * i
        src_low(it, top - GROUP + 1).wait_recv()
        src_high(it, top - GROUP + 1).wait_recv()
        wait_carry(i, e)
        for j in range(GROUP):
            k = top - j

            def load(r, j=j, k=k):
                if j == 0:
                    old = three(carryn, carry, carrys, (e,), r)
                else:
                    old = work[0, r]
                return old + three(srcn, src, srcs, (it, k), r)

            low, high = 2 * j, ROWS - 2 * j
            adjoint_step(load, keep(1), k, low, high)
            adjoint_step(lambda r: work[1, r], keep(0), k, low + 1, high - 1)
            if j == GROUP - 1:

                @pl.when(i < groups - 1)
                def _():
                    carry[e + 1] = work[0, HALO : HALO + LAT]

                send_carry(i, e + 1)
            done(k)

    lax.fori_loop(0, windows, coef_forward, 0)

    def prepare(i):
        for j in range(GROUP):
            k = windows - 1 - GROUP * i - j
            from_peer(obsall, ob2_r, k, None)
            make_hot(k)
            scatter(0, k, obsall[k, 3:4, :] * (0.0 - obsall[k, 2:3, :]))
        src_low(0, k).start()
        src_high(0, k).start()
        for j in range(GROUP):
            expand(windows - 1 - GROUP * i - j)

    prepare(0)

    def first(i, token):
        @pl.when(i < groups - 1)
        def _():
            prepare(i + 1)

        def done(k):
            from_peer(bvr, bv_r, k, bv_own)
            inc[k] = -0.5 * (bvr[k] * work[0, HALO : HALO + LAT])

        adjoint_group(0, i, done)
        k = windows - GROUP - GROUP * i
        inc_low(k).start()
        inc_high(k).start()
        return token

    lax.fori_loop(0, groups, first, 0)

    def observe(i):
        for j in range(GROUP):
            k = GROUP * i + j
            parts = split3(states[k].reshape(cells, LANES))
            picked = jnp.dot(
                jnp.concatenate([part.astype(BF16) for part in parts], axis=0),
                hot[k],
                preferred_element_type=F32,
            )
            total = picked[2 * cells :] + picked[cells : 2 * cells] + picked[:cells]
            seen = jnp.sum(jnp.where(row_mask(k), total, 0.0), axis=0, keepdims=True)
            rel = lane_of(k)
            own = (rel >= margin) & (rel < margin + chunk)
            innov[k] = jnp.where(own, obsall[k, 3:4, :] * (seen - obsall[k, 2:3, :]), 0.0)
        innov_left(GROUP * i).start()
        innov_right(GROUP * i).start()

    def second(i, token):
        @pl.when(i > 0)
        def _():
            observe(i - 1)

        e = groups + i
        inc_low(GROUP * i).wait_recv()
        inc_high(GROUP * i).wait_recv()
        wait_carry(i, e)
        for j in range(GROUP):
            k = GROUP * i + j

            def load(r, j=j, k=k):
                if j == 0:
                    old = three(carryn, carry, carrys, (e,), r)
                else:
                    old = work[0, r]
                total = old + three(incn, inc, incs, (k,), r)
                if r < HALO:
                    return total * edge_low
                if r >= HALO + LAT:
                    return total * edge_high
                return total

            low, high = 2 * j, ROWS - 2 * j
            forward_step(load, keep(1), k, low, high)
            forward_step(lambda r: work[1, r], keep(0), k, low + 1, high - 1)
            if j == GROUP - 1:

                @pl.when(i < groups - 1)
                def _():
                    carry[e + 1] = work[0, HALO : HALO + LAT]

                send_carry(i, e + 1)
            states[k] = work[0, HALO : HALO + LAT]
        return token

    lax.fori_loop(0, groups, second, 0)
    observe(groups - 1)

    def regrid(i):
        k = windows - GROUP - GROUP * i
        innov_left(k).wait_recv()
        innov_right(k).wait_recv()
        for j in range(GROUP):
            scatter(1, k + j, innov[k + j] + innovl[k + j] + innovr[k + j])
        src_low(1, k).start()
        src_high(1, k).start()

    regrid(0)

    def out_copy(k):
        return remote(final.at[k], out_ref.at[m], out_s.at[k], out_r.at[m], (k, t))

    out_own = pltpu.make_async_copy(final.at[m], out_ref.at[m], out_s.at[m])

    def third(i, token):
        @pl.when(i < groups - 1)
        def _():
            regrid(i + 1)

        def done(k):
            old = inc[k]
            final[k] = old - 0.5 * (old + bvr[k] * work[0, HALO : HALO + LAT])

            @pl.when(k != m)
            def _():
                out_copy(k).start()

            @pl.when(k == m)
            def _():
                out_own.start()

        adjoint_group(1, i, done)
        return token

    lax.fori_loop(0, groups, third, 0)

    def finish_obs(d, token):
        obs_copy(d).wait_send()
        return token

    lax.fori_loop(1, tiles, finish_obs, 0)

    def finish_tm(d, token):
        coef_copy(d).wait_send()
        bv_copy(d).wait_send()
        ob2_copy(d).wait_send()
        return token

    lax.fori_loop(1, windows, finish_tm, 0)

    def finish_windows(k, token):
        coef_low(k).wait_send()
        coef_high(k).wait_send()

        @pl.when(k != m)
        def _():
            out_copy(k).wait_send()
            remote(final.at[k], out_ref.at[k], out_s.at[k], out_r.at[k], (k, t)).wait_recv()

        @pl.when(k == m)
        def _():
            out_own.wait()

        return token

    lax.fori_loop(0, windows, finish_windows, 0)

    def finish_groups(i, token):
        k = GROUP * i
        for it in range(2):
            src_low(it, k).wait_send()
            src_high(it, k).wait_send()
        inc_low(k).wait_send()
        inc_high(k).wait_send()
        innov_left(k).wait_send()
        innov_right(k).wait_send()

        @pl.when(i > 0)
        def _():
            for sweep in range(3):
                carry_low(sweep * groups + i).wait_send()
                carry_high(sweep * groups + i).wait_send()

        return token

    lax.fori_loop(0, groups, finish_groups, 0)


def per_device(
    advect_east, advect_north, diffusion, background_var, obs_cell, obs_value, obs_weight, obs_count
):
    windows = lax.axis_size("tm")
    tiles = lax.axis_size("tile")
    groups = windows // GROUP
    chunk = LON // windows
    margin = (LANES - chunk) // 2
    slots = tiles * CAP
    tile = lax.axis_index("tile")

    def chunks(array):
        wide = jnp.concatenate([array[..., -margin:], array, array[..., :margin]], axis=-1)
        return jnp.stack([wide[..., c * chunk : c * chunk + LANES] for c in range(windows)])

    coefs = jnp.stack([advect_east[0], advect_north[0], diffusion[0]])
    coefs = chunks(coefs.transpose(2, 0, 1, 3).reshape(LAT * 6, LON))
    coefs = coefs.reshape(windows, LAT * 6 // 8, 8, LANES)
    variances = chunks(background_var[0].transpose(2, 1, 0, 3).reshape(LAT, FIELDS, LON))

    cell = obs_cell.reshape(tiles, CAP)
    live = jnp.arange(CAP, dtype=jnp.int32)[None, :] < obs_count.reshape(tiles)[:, None]
    masked = obs_weight.reshape(tiles, CAP) * live.astype(F32)
    row, lon = cell // LON, cell % LON
    variable, level, latitude = row // (2 * LAT), row // LAT % 2, row % LAT
    place = latitude * FIELDS + level * (FIELDS // 2) + variable
    packed = jnp.stack(
        [place.astype(F32), lon.astype(F32), obs_value.reshape(tiles, CAP), masked], axis=1
    )
    quarter = jnp.arange(128, dtype=jnp.int32) // CAP == lax.rem(tile, 4)
    packed = jnp.where(quarter, jnp.tile(packed, (1, 1, 128 // CAP)), 0.0)

    field = (FIELDS, LANES)
    dma = pltpu.SemaphoreType.DMA
    out = pl.pallas_call(
        functools.partial(kernel, windows, tiles),
        out_shape=jax.ShapeDtypeStruct((windows, LAT) + field, F32),
        in_specs=[
            pl.BlockSpec(memory_space=pl.ANY),
            pl.BlockSpec(memory_space=pl.ANY),
            pl.BlockSpec(memory_space=pltpu.VMEM),
        ],
        out_specs=pl.BlockSpec(memory_space=pl.ANY),
        scratch_shapes=[
            pltpu.VMEM((tiles, 4, 128), F32),
            pltpu.VMEM((windows, 4, slots), F32),
            pltpu.VMEM((windows, LAT * 6 // 8, 8, LANES), F32),
            pltpu.VMEM((windows, HALO * 6 // 8, 8, LANES), F32),
            pltpu.VMEM((windows, HALO * 6 // 8, 8, LANES), F32),
            pltpu.VMEM((windows, 5, ROWS) + field, F32),
            pltpu.VMEM((windows, LAT) + field, F32),
            pltpu.VMEM((windows, LANES, slots), BF16),
            pltpu.VMEM((2, windows, LAT) + field, F32),
            pltpu.VMEM((2, windows, HALO) + field, F32),
            pltpu.VMEM((2, windows, HALO) + field, F32),
            pltpu.VMEM((windows, LAT) + field, F32),
            pltpu.VMEM((windows, HALO) + field, F32),
            pltpu.VMEM((windows, HALO) + field, F32),
            pltpu.VMEM((windows, LAT) + field, F32),
            pltpu.VMEM((windows, LAT) + field, F32),
            pltpu.VMEM((3 * groups, LAT) + field, F32),
            pltpu.VMEM((3 * groups, HALO) + field, F32),
            pltpu.VMEM((3 * groups, HALO) + field, F32),
            pltpu.VMEM((2, ROWS) + field, F32),
            pltpu.VMEM((windows, 1, slots), F32),
            pltpu.VMEM((windows, 1, slots), F32),
            pltpu.VMEM((windows, 1, slots), F32),
            dma((tiles,)),
            dma((tiles,)),
            dma((windows,)),
            dma((windows,)),
            dma((windows,)),
            dma((windows,)),
            dma((2, windows)),
            dma((2, windows)),
            dma((windows,)),
            dma((windows,)),
            dma((2, 2, groups)),
            dma((2, 2, groups)),
            dma((2, groups)),
            dma((2, groups)),
            dma((2, 3 * groups)),
            dma((2, 3 * groups)),
            dma((2, groups)),
            dma((2, groups)),
            dma((windows,)),
            dma((windows,)),
        ],
        compiler_params=pltpu.CompilerParams(
            collective_id=0, has_side_effects=True, vmem_limit_bytes=48 * 1024 * 1024
        ),
    )(coefs, variances, packed)
    own = out[..., margin : margin + chunk].reshape(windows, LAT, 2, 4, chunk)
    return own.transpose(3, 2, 1, 0, 4).reshape(1, 4, 2, LAT, LON)


def solution(mesh):
    return jax.shard_map(
        per_device,
        mesh=mesh,
        in_specs=(
            P("tm", None, "tile", None),
            P("tm", None, "tile", None),
            P("tm", None, "tile", None),
            P("tm", None, None, "tile", None),
            P("tm", "tile", None),
            P("tm", "tile", None),
            P("tm", "tile", None),
            P("tm", "tile", None),
        ),
        out_specs=P("tm", None, None, "tile", None),
        check_vma=False,
    )
```

time: 853 us -> 109 us (0.13); the launches traced: 838 us -> 109 us
  starting transfers between devices: 384 us -> 0 us
  waiting for transfers between devices: 346 us -> 0 us
  Pallas kernels: 0 us -> 96.7 us
  other arithmetic: 56.7 us -> 2.14 us
  local copies, waits for them, and re-layouts: 47.9 us -> 10.1 us
    ppermute x119 -> x0, starting transfers between devices: 366 us -> none  [the longest x49 226 us: padded(): lax.ppermute(lax.slice_in_dim(block, block.shape[dim] - width, None, axis...]
    ppermute x119 -> x0, waiting for transfers between devices: 333 us -> none  [the longest x21 191 us: shifted(): lax.ppermute(value, axis, [(source, source + steps) for source in range(f...]
    pallas_call x0 -> x1, Pallas kernels: none -> 96.7 us  [per_device(): pl.pallas_call(functools.partial(kernel, windows, tiles), out_shape=jax.S...]
    add x67 -> x0, other arithmetic: 30.8 us -> none  [the longest x30 15.7 us: apply_step(): middle + jnp.roll(to_east[:, :, 1:-1], 1, axis=-1)]
    slice x212 -> x3, local copies, waits for them, and re-layouts: 23.8 us -> 0.42 us  [the longest x1 0.27 us: per_device(): own = out[..., margin:margin + chunk].reshape(windows, LAT, 2, 4, chunk)]
    all_to_all x2 -> x0, starting transfers between devices: 17.6 us -> none  [the longest x1 13 us: per_device(): lax.all_to_all(cells, 'tile', split_axis=0, concat_axis=0, tiled=True)]
    all_to_all x2 -> x0, waiting for transfers between devices: 12.5 us -> none  [the longest x1 7.94 us: per_device(): lax.all_to_all(jnp.stack([obs_value.reshape(tiles, -1), masked]), 'tile',...]
    scatter-add x2 -> x0, other arithmetic: 12.1 us -> none  [per_device(): gridded = jnp.zeros((cell_total,), jnp.float32).at[flat_cells].add(innov)]
  transfers between devices with their start and end apart: 121 -> 0, of which waited for: 71 -> 0; matrix products, arithmetic and copies ran while one was open for 2% -> 0% of each run, Pallas kernels for 0% -> 0%
where the time goes in v1:
time: 109 us
  Pallas kernels  96.7 us (89%)
  local copies, waits for them, and re-layouts  10.1 us (9%)
  other arithmetic  2.14 us (2%)
    pallas_call x1, Pallas kernels, per_device(): pl.pallas_call(functools.partial(kernel, windows, tiles), out_shape=jax.S...  96.7 us
    unnamed x27, local copies, waits for them, and re-layouts  4.58 us

profile of v1, /device:TPU:1, one launch (start us, length us, event | category | flops | bytes accessed | tf_op | source)
XLA Modules:
  0.0 109.1 jit_solution(9348357996934630800)
XLA Ops:
  0.0 1.4 %copy.13 = f32[12,2,4,1440]{3,2,1,0:T(4,128)S(1)} copy(f32[12,2,4,1440]{3,1,0,2:T(2,128)} %bitcast.78) | data formatting | bytes 1105920 | tf_op jit(solution)/shard_map/transpose | solution.py:622
  1.4 0.2 reshape.257
  1.7 0.1 fusion.30
  1.7 0.1 fusion.9
  1.8 0.1 fusion.7
  1.9 0.1 fusion.6
  2.0 0.1 fusion.5
  2.1 0.1 fusion.4
  2.2 0.1 fusion.3
  2.3 0.1 fusion.2
  2.4 0.0 copy-start
  2.4 0.0 copy-start.1
  2.4 0.0 copy-start.2
  2.4 0.1 fusion.1.bv_in
  2.6 0.8 copy-done
  3.3 0.1 copy-done.1
  3.4 0.1 copy-done.2
  3.5 0.2 maximum_bitcast_fusion
  3.7 0.3 reshape.256
  4.0 0.1 fusion.31
  4.1 0.1 fusion.19
  4.2 0.1 fusion.17
  4.3 0.1 fusion.16
  4.4 0.1 fusion.15
  4.5 0.1 fusion.14
  4.5 0.1 fusion.13
  4.6 0.1 fusion.12
  4.7 0.1 fusion.11.coef_in
  4.9 0.7 copy-done.3
  5.6 0.1 div.49
  5.6 0.1 rem.105
  5.7 0.1 ne.140
  5.8 0.1 fusion.23
  5.9 0.5 broadcast.252
  6.4 0.2 copy-done.4
  6.6 0.7 reduce.16
  7.2 0.1 reshape.258
  7.3 0.7 copy-done.6
  8.0 0.1 fusion.28
  8.0 0.6 copy-done.5
  8.7 0.7 reduce.17
  9.3 0.1 stack_reshape.3
  9.5 0.2 tile.10
  9.7 96.7 %shard_map.82 = f32[8,12,8,256]{3,2,1,0:T(8,128)S(1)} custom-call(f32[8,9,8,256]{3,2,1,0:T(8,128)S(1)} %fusion.11.coef_in, f32[8,12,8,256]{3,2,1,0:T(8,128)S(1)} %fusion.1.bv_in, f32[32,4,128]{2,1,0:T(4,128)S(1)} %broadcast_select_fusion.obs_in), custom_call_target="tpu_custom_call" | custom-call | tf_op jit(solution)/shard_map/pallas_call | solution.py:638
  106.4 0.3 slice.87
  106.7 0.2 reshape.259
  106.9 0.5 copy.15
  107.4 1.7 %reshape.260 = f32[1,4,2,12,1440]{4,2,3,1,0:T(2,128)} reshape(f32[4,2,12,8,180]{4,3,1,2,0:T(8,128)S(1)} %copy.15) | data formatting | bytes 1105920 | tf_op jit(solution)/shard_map/reshape | solution.py:697
  (12 shorter events, 0.2 us)
Async XLA Ops:
  2.4 0.9 copy-start
  2.4 1.0 copy-start.1
  2.4 1.0 copy-start.2
  4.8 0.7 copy-start.3
  5.9 0.7 copy-start.4
  7.3 0.7 copy-start.6
  8.0 0.7 copy-start.5

commit v2 on v1

v2 whole, which is shorter than its diff:
```python
import functools

import jax
import jax.numpy as jnp
from jax import lax
from jax.experimental import pallas as pl
from jax.experimental.pallas import tpu as pltpu
from jax.sharding import PartitionSpec as P

MESH = pl.DeviceIdType.MESH
F32 = jnp.float32
BF16 = jnp.bfloat16
LON = 1440
LAT = 12
CAP = 32
FIELDS = 8
LANES = 256
GROUP = 4
HALO = 2 * GROUP
ROWS = LAT + 2 * HALO
REACH = [max(2 * (GROUP - j) - 1, 2 * (j + 1)) for j in range(GROUP)]


def split3(value):
    high = value.astype(BF16).astype(F32)
    rest = value - high
    middle = rest.astype(BF16).astype(F32)
    return high, middle, rest - middle


def kernel(
    windows,
    tiles,
    coef_in,
    bv_in,
    cell_in,
    value_in,
    weight_in,
    count_in,
    out_ref,
    obs0,
    obs1,
    obsall,
    craw,
    crawn,
    craws,
    der,
    bvraw,
    bvpack,
    bvr,
    hot,
    src,
    inc,
    incn,
    incs,
    states,
    final,
    carry,
    carryn,
    carrys,
    result,
    work,
    innov,
    arrived,
    obs_s,
    obs_r,
    ob2_s,
    ob2_r,
    c_s,
    c_r,
    ch_s,
    ch_r,
    raw_s,
    bv_s,
    bv_r,
    inc_s,
    inc_r,
    car_s,
    car_r,
    inn_s,
    inn_r,
    out_s,
    out_r,
):
    m = lax.axis_index("tm")
    t = lax.axis_index("tile")
    chunk = LON // windows
    margin = (LANES - chunk) // 2
    groups = windows // GROUP
    slots = obsall.shape[-1]
    cells = LAT * FIELDS
    up = lax.rem(t + 1, tiles)
    down = lax.rem(t + tiles - 1, tiles)
    left = lax.rem(m + windows - 1, windows)
    right = lax.rem(m + 1, windows)
    edge_low = jnp.where(t == 0, 0.0, 1.0).astype(F32)
    edge_high = jnp.where(t == tiles - 1, 0.0, 1.0).astype(F32)

    barrier = pltpu.get_barrier_semaphore()

    def greet_tile(d, token):
        pl.semaphore_signal(
            barrier, inc=1, device_id=(m, lax.rem(t + d, tiles)), device_id_type=MESH
        )
        return token

    def greet_tm(d, token):
        for where in (t, down, up):
            pl.semaphore_signal(
                barrier, inc=1, device_id=(lax.rem(m + d, windows), where), device_id_type=MESH
            )
        return token

    lax.fori_loop(1, tiles, greet_tile, 0)
    lax.fori_loop(1, windows, greet_tm, 0)

    raw_copy = pltpu.make_async_copy(bv_in, bvraw, raw_s)
    raw_copy.start()
    lane = lax.broadcasted_iota(jnp.int32, (1, 128), 1)
    quarter = lane // CAP
    slot = lane - CAP * quarter
    mine = lax.rem(t, 4)

    def floor_div(value, by):
        return jnp.floor((value + 0.5) * (1.0 / by))

    for a in range(tiles // 4):
        part = slice(a * 128, (a + 1) * 128)
        cell = cell_in[0:1, part].astype(F32)
        row = floor_div(cell, LON)
        lon = cell - LON * row
        variable = floor_div(row, 2 * LAT)
        rest = row - 2 * LAT * variable
        level = floor_div(rest, LAT)
        place = FIELDS * (rest - LAT * level) + 2 * variable + level
        filled = jnp.where(
            quarter < 2,
            jnp.where(quarter == 0, count_in[0, 4 * a], count_in[0, 4 * a + 1]),
            jnp.where(quarter == 2, count_in[0, 4 * a + 2], count_in[0, 4 * a + 3]),
        )
        weight = jnp.where(slot < filled, weight_in[0:1, part], 0.0)
        block = jnp.concatenate(
            [place * LON + lon, value_in[0:1, part], weight, jnp.zeros((1, 128), F32)], axis=0
        )
        for b in range(4):
            turned = pltpu.roll(block, CAP * lax.rem(mine + 4 - b, 4), 1)
            obs0[4 * a + b] = jnp.where(quarter == mine, turned, 0.0)

    for ref in (carry, carryn, carrys):
        for sweep in range(3):
            ref[sweep * groups] = jnp.zeros(ref.shape[1:], F32)

    pl.semaphore_wait(barrier, tiles - 1 + 3 * (windows - 1))

    def remote(source, target, send, recv, where):
        return pltpu.make_async_remote_copy(
            src_ref=source,
            dst_ref=target,
            send_sem=send,
            recv_sem=recv,
            device_id=where,
            device_id_type=MESH,
        )

    def obs_copy(d):
        peer = lax.rem(t + d, tiles)
        return remote(obs0.at[peer], obs1.at[t], obs_s.at[d], obs_r.at[d], (m, peer))

    def obs_start(d, token):
        obs_copy(d).start()
        return token

    lax.fori_loop(1, tiles, obs_start, 0)

    coef_own = pltpu.make_async_copy(coef_in.at[m], craw.at[m], c_s.at[0])
    coef_own.start()

    def coef_copy(d):
        peer = lax.rem(m + d, windows)
        return remote(coef_in.at[peer], craw.at[m], c_s.at[d], c_r.at[m], (peer, t))

    def bv_copy(d):
        peer = lax.rem(m + d, windows)
        return remote(bvpack.at[peer], bvr.at[m], bv_s.at[d], bv_r.at[m], (peer, t))

    def coef_start(d, token):
        coef_copy(d).start()
        return token

    lax.fori_loop(1, windows, coef_start, 0)

    raw_copy.wait()
    for c in range(windows):
        start = c * chunk - margin
        for r in range(LAT):
            if start < 0:
                piece = jnp.concatenate(
                    [bvraw[:, r, LON + start : LON], bvraw[:, r, 0 : LANES + start]], axis=1
                )
            elif start + LANES > LON:
                piece = jnp.concatenate(
                    [bvraw[:, r, start:LON], bvraw[:, r, 0 : start + LANES - LON]], axis=1
                )
            else:
                piece = bvraw[:, r, start : start + LANES]
            bvpack[c, r] = piece
    bvr[m] = bvpack[m]

    obs1[t] = obs0[t]

    def obs_wait(d, token):
        obs_copy(d).wait_recv()
        return token

    lax.fori_loop(1, tiles, obs_wait, 0)
    for j in range(tiles // 4):
        merged = obs1[4 * j] + obs1[4 * j + 1] + obs1[4 * j + 2] + obs1[4 * j + 3]
        for c in range(3):
            obsall[m, 0, c, :, j * 128 : (j + 1) * 128] = merged[c : c + 1]

    def ob2_copy(d, n):
        peer = lax.rem(m + d, windows)
        where = (t, up, down)[n]
        return remote(
            obsall.at[m, 0], obsall.at[m, n], ob2_s.at[n, d], ob2_r.at[n, m], (peer, where)
        )

    def ob2_start(d, token):
        for n in range(3):
            ob2_copy(d, n).start()
        return token

    for n in (1, 2):
        ob2_copy(0, n).start()
    lax.fori_loop(1, windows, ob2_start, 0)

    def bv_start(d, token):
        bv_copy(d).start()
        return token

    lax.fori_loop(1, windows, bv_start, 0)

    def from_peer(ref, sem, k, own):
        @pl.when(k != m)
        def _():
            remote(ref.at[k], ref.at[k], sem.at[k], sem.at[k], (k, t)).wait_recv()

        if own is not None:

            @pl.when(k == m)
            def _():
                own.wait()

    whole = LAT * 6 // 8
    edge_tiles = HALO * 6 // 8

    def coef_low(k, j):
        size = -(-REACH[j] * 6 // 8)
        return remote(
            craw.at[k, 0:size], craws.at[k, 0:size], ch_s.at[0, k], ch_r.at[0, k], (m, down)
        )

    def coef_high(k, j):
        size = -(-REACH[j] * 6 // 8)
        return remote(
            craw.at[k, whole - size : whole],
            crawn.at[k, edge_tiles - size : edge_tiles],
            ch_s.at[1, k],
            ch_r.at[1, k],
            (m, up),
        )

    def coef_forward(i, token):
        for j in range(GROUP - 1, -1, -1):
            k = windows - GROUP - GROUP * i + j
            from_peer(craw, c_r, k, coef_own)
            coef_low(k, j).start()
            coef_high(k, j).start()
        return token

    even = lax.rem(lax.broadcasted_iota(jnp.int32, (FIELDS, LANES), 0), 2) == 0

    def expand(k, j):
        coef_low(k, j).wait_recv()
        coef_high(k, j).wait_recv()
        for r in range(HALO - REACH[j], HALO + LAT + REACH[j]):
            if r < HALO:
                ref, row, edge = crawn, r, edge_low
            elif r < HALO + LAT:
                ref, row, edge = craw, r - HALO, None
            else:
                ref, row, edge = craws, r - HALO - LAT, edge_high
            picked = []
            for c in range(3):
                q = (row * 3 + c) * 2
                one = ref[k, q // 8, q % 8 : q % 8 + 1, :]
                two = ref[k, q // 8, q % 8 + 1 : q % 8 + 2, :]
                picked.append(
                    jnp.where(
                        even,
                        jnp.broadcast_to(one, (FIELDS, LANES)),
                        jnp.broadcast_to(two, (FIELDS, LANES)),
                    )
                )
            half_east, half_north, kap = 0.5 * picked[0], 0.5 * picked[1], picked[2]
            made = (
                1.0 - 4.0 * kap,
                kap - half_east,
                kap + half_east,
                kap - half_north,
                kap + half_north,
            )
            for c in range(5):
                der[k, c, r] = made[c] if edge is None else made[c] * edge

    base = m * chunk - margin

    def place_and_lane(k, n):
        code = obsall[k, n, 0]
        place = floor_div(code, LON)
        rel = (code - LON * place).astype(jnp.int32) - base
        rel = jnp.where(rel >= LON, rel - LON, rel)
        return place.astype(jnp.int32), jnp.where(rel < 0, rel + LON, rel)

    def make_hot(k, n):
        place, rel = place_and_lane(k, n)
        lanes = lax.broadcasted_iota(jnp.int32, (LANES, slots), 0)
        hot[k, n] = jnp.where(lanes == rel, 1.0, 0.0).astype(BF16)

    def row_mask(k, n, first, count):
        place, rel = place_and_lane(k, n)
        rows = lax.broadcasted_iota(jnp.int32, (count * FIELDS, slots), 0) + first * FIELDS
        return rows == place

    def scatter(it, k, j, value_of):
        reach = 2 * (j + 1)
        for n, first, count, to in (
            (0, 0, LAT, HALO),
            (1, LAT - reach, reach, HALO - reach),
            (2, 0, reach, HALO + LAT),
        ):
            mask = row_mask(k, n, first, count)
            parts = [jnp.where(mask, part, 0.0).astype(BF16) for part in split3(value_of(n))]
            sums = lax.dot_general(
                jnp.concatenate(parts, axis=0),
                hot[k, n],
                (((1,), (1,)), ((), ())),
                preferred_element_type=F32,
            )
            size = count * FIELDS
            total = sums[2 * size :] + sums[size : 2 * size] + sums[:size]
            src[it, k, to : to + count] = total.reshape(count, FIELDS, LANES)

    def inc_low(k, j):
        size = HALO - 2 * j
        return remote(
            inc.at[k, 0:size], incs.at[k, 0:size], inc_s.at[0, k], inc_r.at[0, k], (m, down)
        )

    def inc_high(k, j):
        size = HALO - 2 * j
        return remote(
            inc.at[k, LAT - size : LAT],
            incn.at[k, HALO - size : HALO],
            inc_s.at[1, k],
            inc_r.at[1, k],
            (m, up),
        )

    def carry_low(e):
        return remote(
            carry.at[e, 0:HALO], carrys.at[e], car_s.at[0, e], car_r.at[0, e], (m, down)
        )

    def carry_high(e):
        return remote(
            carry.at[e, LAT - HALO : LAT], carryn.at[e], car_s.at[1, e], car_r.at[1, e], (m, up)
        )

    steps = [(a, b) for a in (0, -1, 1) for b in (0, 1, -1)][1:]

    def innov_copy(k, n):
        a, b = steps[n]
        return remote(
            innov.at[pl.ds(k, GROUP)],
            arrived.at[n, pl.ds(k, GROUP)],
            inn_s.at[n, k // GROUP],
            inn_r.at[n, k // GROUP],
            ((left, m, right)[a + 1], (down, t, up)[b + 1]),
        )

    def three(north, own, south, index, r):
        if r < HALO:
            return north[index + (r,)]
        if r < HALO + LAT:
            return own[index + (r - HALO,)]
        return south[index + (r - HALO - LAT,)]

    def adjoint_step(load, store, k, low, high):
        to_next = None
        held = None
        for r in range(low, high):
            x = load(r)
            south = der[k, 4, r] * x
            if held is not None and r - 1 >= low + 1:
                store(r - 1, held + south)
            if r < high - 1 and r > low:
                held = (
                    der[k, 0, r] * x
                    + pltpu.roll(der[k, 1, r] * x, 1, 1)
                    + pltpu.roll(der[k, 2, r] * x, LANES - 1, 1)
                    + to_next
                )
            to_next = der[k, 3, r] * x

    def forward_step(load, store, k, low, high):
        before, here = load(low), load(low + 1)
        for r in range(low + 1, high - 1):
            after = load(r + 1)
            store(
                r,
                der[k, 0, r] * here
                + der[k, 1, r] * pltpu.roll(here, LANES - 1, 1)
                + der[k, 2, r] * pltpu.roll(here, 1, 1)
                + der[k, 3, r] * after
                + der[k, 4, r] * before,
            )
            before, here = here, after

    def keep(slot):
        def store(r, value):
            work[slot, r] = value

        return store

    def wait_carry(i, e):
        @pl.when(i > 0)
        def _():
            carry_low(e).wait_recv()
            carry_high(e).wait_recv()

    def send_carry(i, e):
        @pl.when(i < groups - 1)
        def _():
            carry_low(e).start()
            carry_high(e).start()

    def adjoint_group(it, i, done):
        e = 2 * it * groups + i
        top = windows - 1 - GROUP * i
        wait_carry(i, e)
        for j in range(GROUP):
            k = top - j

            def load(r, j=j, k=k):
                if j == 0:
                    old = three(carryn, carry, carrys, (e,), r)
                else:
                    old = work[0, r]
                return old + src[it, k, r]

            low, high = 2 * j, ROWS - 2 * j
            adjoint_step(load, keep(1), k, low, high)
            adjoint_step(lambda r: work[1, r], keep(0), k, low + 1, high - 1)
            if j == GROUP - 1:

                @pl.when(i < groups - 1)
                def _():
                    carry[e + 1] = work[0, HALO : HALO + LAT]

                send_carry(i, e + 1)
            done(k)

    lax.fori_loop(0, groups, coef_forward, 0)

    def prepare(i):
        for j in range(GROUP - 1, -1, -1):
            k = windows - GROUP - GROUP * i + j
            for n in range(3):
                sem = ob2_r.at[n, k]
                if n == 0:

                    @pl.when(k != m)
                    def _(k=k, sem=sem):
                        remote(
                            obsall.at[k, 0], obsall.at[k, 0], sem, sem, (k, t)
                        ).wait_recv()

                else:
                    remote(
                        obsall.at[k, n], obsall.at[k, n], sem, sem, (k, (down, up)[n - 1])
                    ).wait_recv()
                make_hot(k, n)
            scatter(0, k, j, lambda n, k=k: obsall[k, n, 2] * (0.0 - obsall[k, n, 1]))
        for j in range(GROUP - 1, -1, -1):
            expand(windows - GROUP - GROUP * i + j, j)

    prepare(0)

    def increments(i):
        for j in range(GROUP):
            k = windows - GROUP - GROUP * i + j
            from_peer(bvr, bv_r, k, None)
            inc[k] = -0.5 * (bvr[k] * inc[k])
            inc_low(k, j).start()
            inc_high(k, j).start()

    def first(i, token):
        @pl.when(i < groups - 1)
        def _():
            prepare(i + 1)

        @pl.when(i > 0)
        def _():
            increments(i - 1)

        def done(k):
            inc[k] = work[0, HALO : HALO + LAT]

        adjoint_group(0, i, done)
        return token

    lax.fori_loop(0, groups, first, 0)
    increments(groups - 1)

    def observe(i):
        for j in range(GROUP):
            k = GROUP * i + j
            parts = split3(states[k].reshape(cells, LANES))
            picked = jnp.dot(
                jnp.concatenate([part.astype(BF16) for part in parts], axis=0),
                hot[k, 0],
                preferred_element_type=F32,
            )
            total = picked[2 * cells :] + picked[cells : 2 * cells] + picked[:cells]
            seen = jnp.sum(jnp.where(row_mask(k, 0, 0, LAT), total, 0.0), axis=0, keepdims=True)
            place, rel = place_and_lane(k, 0)
            own = (rel >= margin) & (rel < margin + chunk)
            innov[k] = jnp.where(own, obsall[k, 0, 2] * (seen - obsall[k, 0, 1]), 0.0)
        for n in range(8):
            innov_copy(GROUP * i, n).start()

    def second(i, token):
        @pl.when(i > 0)
        def _():
            observe(i - 1)

        e = groups + i
        wait_carry(i, e)
        for j in range(GROUP):
            k = GROUP * i + j
            inc_low(k, j).wait_recv()
            inc_high(k, j).wait_recv()

            def load(r, j=j, k=k):
                if j == 0:
                    old = three(carryn, carry, carrys, (e,), r)
                else:
                    old = work[0, r]
                total = old + three(incn, inc, incs, (k,), r)
                if r < HALO:
                    return total * edge_low
                if r >= HALO + LAT:
                    return total * edge_high
                return total

            low, high = 2 * j, ROWS - 2 * j
            forward_step(load, keep(1), k, low, high)
            forward_step(lambda r: work[1, r], keep(0), k, low + 1, high - 1)
            if j == GROUP - 1:

                @pl.when(i < groups - 1)
                def _():
                    carry[e + 1] = work[0, HALO : HALO + LAT]

                send_carry(i, e + 1)
            states[k] = work[0, HALO : HALO + LAT]
        return token

    lax.fori_loop(0, groups, second, 0)
    observe(groups - 1)

    def regrid(i):
        k = windows - GROUP - GROUP * i
        for n in range(8):
            innov_copy(k, n).wait_recv()

        def total(n, k):
            b = (0, 1, -1)[n]
            found = [arrived[x, k] for x in range(8) if steps[x][1] == b]
            if n == 0:
                found.append(innov[k])
            return found[0] + found[1] + found[2]

        for j in range(GROUP - 1, -1, -1):
            scatter(1, k + j, j, lambda n, k=k + j: total(n, k))

    regrid(0)

    def out_copy(k):
        return remote(final.at[k], result.at[m], out_s.at[k], out_r.at[m], (k, t))


    def third(i, token):
        @pl.when(i < groups - 1)
        def _():
            regrid(i + 1)

        def done(k):
            old = inc[k]
            final[k] = old - 0.5 * (old + bvr[k] * work[0, HALO : HALO + LAT])

            @pl.when(k != m)
            def _():
                out_copy(k).start()

            @pl.when(k == m)
            def _():
                result[k] = final[k]

        adjoint_group(1, i, done)
        return token

    lax.fori_loop(0, groups, third, 0)

    def finish_obs(d, token):
        obs_copy(d).wait_send()
        return token

    lax.fori_loop(1, tiles, finish_obs, 0)

    def finish_tm(d, token):
        coef_copy(d).wait_send()
        bv_copy(d).wait_send()
        for n in range(3):
            ob2_copy(d, n).wait_send()
        return token

    for n in (1, 2):
        ob2_copy(0, n).wait_send()
    lax.fori_loop(1, windows, finish_tm, 0)

    def finish_groups(i, token):
        for j in range(GROUP):
            k = GROUP * i + j
            coef_low(k, j).wait_send()
            coef_high(k, j).wait_send()
            inc_low(k, j).wait_send()
            inc_high(k, j).wait_send()
        for n in range(8):
            innov_copy(GROUP * i, n).wait_send()

        @pl.when(i > 0)
        def _():
            for sweep in range(3):
                carry_low(sweep * groups + i).wait_send()
                carry_high(sweep * groups + i).wait_send()

        return token

    lax.fori_loop(0, groups, finish_groups, 0)

    def finish_windows(k, token):
        @pl.when(k != m)
        def _():
            remote(final.at[k], result.at[k], out_s.at[k], out_r.at[k], (k, t)).wait_recv()
            out_copy(k).wait_send()

        return token

    lax.fori_loop(0, windows, finish_windows, 0)
    for r in range(LAT):
        out_ref[:, r, :] = jnp.concatenate(
            [result[c, r, :, margin : margin + chunk] for c in range(windows)], axis=1
        )


def per_device(
    advect_east, advect_north, diffusion, background_var, obs_cell, obs_value, obs_weight, obs_count
):
    windows = lax.axis_size("tm")
    tiles = lax.axis_size("tile")
    groups = windows // GROUP
    chunk = LON // windows
    margin = (LANES - chunk) // 2
    slots = tiles * CAP

    def chunks(array):
        wide = jnp.concatenate([array[..., -margin:], array, array[..., :margin]], axis=-1)
        return jnp.stack([wide[..., c * chunk : c * chunk + LANES] for c in range(windows)])

    coefs = jnp.stack([advect_east[0], advect_north[0], diffusion[0]])
    coefs = chunks(coefs.transpose(2, 0, 1, 3).reshape(LAT * 6, LON))
    coefs = coefs.reshape(windows, LAT * 6 // 8, 8, LANES)
    field = (FIELDS, LANES)
    dma = pltpu.SemaphoreType.DMA
    out = pl.pallas_call(
        functools.partial(kernel, windows, tiles),
        out_shape=jax.ShapeDtypeStruct((FIELDS, LAT, LON), F32),
        in_specs=[
            pl.BlockSpec(memory_space=pl.ANY),
            pl.BlockSpec(memory_space=pl.ANY),
            pl.BlockSpec(memory_space=pltpu.VMEM),
            pl.BlockSpec(memory_space=pltpu.VMEM),
            pl.BlockSpec(memory_space=pltpu.VMEM),
            pl.BlockSpec(memory_space=pltpu.SMEM),
        ],
        out_specs=pl.BlockSpec(memory_space=pltpu.VMEM),
        scratch_shapes=[
            pltpu.VMEM((tiles, 4, 128), F32),
            pltpu.VMEM((tiles, 4, 128), F32),
            pltpu.VMEM((windows, 3, 3, 1, slots), F32),
            pltpu.VMEM((windows, LAT * 6 // 8, 8, LANES), F32),
            pltpu.VMEM((windows, HALO * 6 // 8, 8, LANES), F32),
            pltpu.VMEM((windows, HALO * 6 // 8, 8, LANES), F32),
            pltpu.VMEM((windows, 5, ROWS) + field, F32),
            pltpu.VMEM((FIELDS, LAT, LON), F32),
            pltpu.VMEM((windows, LAT) + field, F32),
            pltpu.VMEM((windows, LAT) + field, F32),
            pltpu.VMEM((windows, 3, LANES, slots), BF16),
            pltpu.VMEM((2, windows, ROWS) + field, F32),
            pltpu.VMEM((windows, LAT) + field, F32),
            pltpu.VMEM((windows, HALO) + field, F32),
            pltpu.VMEM((windows, HALO) + field, F32),
            pltpu.VMEM((windows, LAT) + field, F32),
            pltpu.VMEM((windows, LAT) + field, F32),
            pltpu.VMEM((3 * groups, LAT) + field, F32),
            pltpu.VMEM((3 * groups, HALO) + field, F32),
            pltpu.VMEM((3 * groups, HALO) + field, F32),
            pltpu.VMEM((windows, LAT) + field, F32),
            pltpu.VMEM((2, ROWS) + field, F32),
            pltpu.VMEM((windows, 1, slots), F32),
            pltpu.VMEM((8, windows, 1, slots), F32),
            dma((tiles,)),
            dma((tiles,)),
            dma((3, windows)),
            dma((3, windows)),
            dma((windows,)),
            dma((windows,)),
            dma((2, windows)),
            dma((2, windows)),
            dma,
            dma((windows,)),
            dma((windows,)),
            dma((2, windows)),
            dma((2, windows)),
            dma((2, 3 * groups)),
            dma((2, 3 * groups)),
            dma((8, groups)),
            dma((8, groups)),
            dma((windows,)),
            dma((windows,)),
        ],
        compiler_params=pltpu.CompilerParams(
            collective_id=0, has_side_effects=True, vmem_limit_bytes=48 * 1024 * 1024
        ),
    )(
        coefs,
        background_var.reshape(FIELDS, LAT, LON),
        obs_cell.reshape(1, slots),
        obs_value.reshape(1, slots),
        obs_weight.reshape(1, slots),
        obs_count.reshape(1, tiles),
    )
    return out.reshape(1, FIELDS // 2, 2, LAT, LON)


def solution(mesh):
    return jax.shard_map(
        per_device,
        mesh=mesh,
        in_specs=(
            P("tm", None, "tile", None),
            P("tm", None, "tile", None),
            P("tm", None, "tile", None),
            P("tm", None, None, "tile", None),
            P("tm", "tile", None),
            P("tm", "tile", None),
            P("tm", "tile", None),
            P("tm", "tile", None),
        ),
        out_specs=P("tm", None, None, "tile", None),
        check_vma=False,
    )
```

time: 109 us -> 86.3 us (0.79)
  Pallas kernels: 96.7 us -> 81.1 us
  local copies, waits for them, and re-layouts: 10.1 us -> 3.58 us
    pallas_call x1, Pallas kernels: 96.7 us -> 81.1 us  [per_device(): pl.pallas_call(functools.partial(kernel, windows, tiles), out_shape=jax.S...]
    unnamed x27 -> x17, local copies, waits for them, and re-layouts: 4.58 us -> 1.89 us
    transpose x2 -> x0, local copies, waits for them, and re-layouts: 1.91 us -> none  [the longest x1 1.45 us: per_device(): background_var[0].transpose(2, 1, 0, 3).reshape(LAT, FIELDS, LON)]
    unnamed x4 -> x1, other arithmetic: 1.5 us -> 0.08 us
    reshape x4 -> x1, local copies, waits for them, and re-layouts: 2.24 us -> 1.27 us  [per_device(): return out.reshape(1, FIELDS // 2, 2, LAT, LON)]
where the time goes in v2:
time: 86.3 us; the launch traced here: 86.2 us
  Pallas kernels  81.1 us (94%)
  local copies, waits for them, and re-layouts  3.58 us (4%)
  other arithmetic  1.45 us (2%)
    pallas_call x1, Pallas kernels, per_device(): pl.pallas_call(functools.partial(kernel, windows, tiles), out_shape=jax.S...  81.1 us
    unnamed x17, local copies, waits for them, and re-layouts  1.89 us

profile of v2, /device:TPU:1, one launch (start us, length us, event | category | flops | bytes accessed | tf_op | source)
XLA Modules:
  0.0 86.2 jit_solution(9175513631395917871)
XLA Ops:
  0.0 1.3 %maximum_bitcast_fusion = f32[12,3,2,1440]{3,2,0,1:T(2,128)S(1)} fusion(f32[1,2,12,1440]{3,1,2,0:T(2,128)} %param.10, f32[1,2,12,1440]{3,1,2,0:T(2,128)} %param.9, f32[1,2,12,1440]{3,1,2,0:T(2,128)} %param.8), kind=kLoop, calls=%fused_computation | loop fusion | flops 207360 | bytes 829440 | tf_op jit(solution)/shard_map/transpose | solution.py:693
  1.3 0.3 reshape.38
  1.6 0.1 fusion.10
  1.7 0.1 fusion.9
  1.8 0.1 fusion.7
  1.9 0.1 fusion.6
  1.9 0.0 copy-start.4
  2.0 0.1 fusion.5
  2.0 0.1 fusion.4
  2.1 0.1 fusion.3
  2.2 0.1 fusion.2
  2.3 0.1 fusion.1.coef_in
  2.4 0.6 copy-done.4
  3.0 0.0 copy-start
  3.0 0.0 copy-start.1
  3.0 0.0 copy-start.2
  3.0 0.1 copy.12
  3.2 0.0 copy-start.3
  3.2 0.5 copy-done
  3.7 0.0 copy-done.1
  3.7 0.0 copy-done.2
  3.7 0.1 copy-done.3
  3.8 81.1 %shard_map.82 = f32[8,12,1440]{2,1,0:T(8,128)S(1)} custom-call(f32[8,9,8,256]{3,2,1,0:T(8,128)S(1)} %fusion.1.coef_in, f32[8,12,1440]{2,1,0:T(8,128)S(1)} %bitcast.41, s32[1,1024]{1,0:T(1,128)S(1)} %bitcast.42, f32[1,1024]{1,0:T(1,128)S(1)} %bitcast.43, f32[1,1024]{1,0:T(1,128)S(1)} %bitcast.44, s32[1,32]{1,0:T(1,128)S(1)} %bitcast.45), custom_call_target="tpu_custom_call" | custom-call | tf_op jit(solution)/shard_map/pallas_call | solution.py:697
  84.9 1.3 %copy.13 = f32[1,4,2,12,1440]{4,2,3,1,0:T(2,128)} copy(f32[1,4,2,12,1440]{4,3,2,1,0:T(8,128)S(1)} %bitcast.40) | data formatting | bytes 1105920 | tf_op jit(solution)/shard_map/reshape | solution.py:765
  (1 shorter events, 0.0 us)
Async XLA Ops:
  1.9 1.1 %copy-start.4 = (f32[1,4,2,12,1440]{4,2,3,1,0:T(2,128)S(1)}, f32[1,4,2,12,1440]{4,2,3,1,0:T(2,128)}, u32[]{:S(2)}) copy-start(f32[1,4,2,12,1440]{4,2,3,1,0:T(2,128)} %param.11) | copy-start | bytes 1658884
  3.0 0.7 copy-start
  3.0 0.7 copy-start.1
  3.0 0.7 copy-start.2
  3.2 0.7 copy-start.3

commit v3 on v2

--- a/solution.py
+++ b/solution.py
@@ -31,13 +31,22 @@
 def kernel(
     windows,
     tiles,
+    east_hbm,
+    north_hbm,
+    diff_hbm,
+    bv_hbm,
+    cell_hbm,
+    value_hbm,
+    weight_hbm,
+    count_hbm,
+    out_ref,
+    coef3,
+    coef72,
     coef_in,
-    bv_in,
     cell_in,
     value_in,
     weight_in,
     count_in,
-    out_ref,
     obs0,
     obs1,
     obsall,
@@ -96,6 +105,24 @@
     edge_low = jnp.where(t == 0, 0.0, 1.0).astype(F32)
     edge_high = jnp.where(t == tiles - 1, 0.0, 1.0).astype(F32)
 
+    fetches = [
+        pltpu.make_async_copy(source, target, raw_s.at[i])
+        for i, (source, target) in enumerate(
+            (
+                (cell_hbm, cell_in),
+                (value_hbm, value_in),
+                (weight_hbm, weight_in),
+                (count_hbm, count_in),
+                (east_hbm, coef3.at[0]),
+                (north_hbm, coef3.at[1]),
+                (diff_hbm, coef3.at[2]),
+                (bv_hbm, bvraw),
+            )
+        )
+    ]
+    for fetch in fetches:
+        fetch.start()
+
     barrier = pltpu.get_barrier_semaphore()
 
     def greet_tile(d, token):
@@ -114,8 +141,6 @@
     lax.fori_loop(1, tiles, greet_tile, 0)
     lax.fori_loop(1, windows, greet_tm, 0)
 
-    raw_copy = pltpu.make_async_copy(bv_in, bvraw, raw_s)
-    raw_copy.start()
     lane = lax.broadcasted_iota(jnp.int32, (1, 128), 1)
     quarter = lane // CAP
     slot = lane - CAP * quarter
@@ -124,6 +149,8 @@
     def floor_div(value, by):
         return jnp.floor((value + 0.5) * (1.0 / by))
 
+    for fetch in fetches[:4]:
+        fetch.wait()
     for a in range(tiles // 4):
         part = slice(a * 128, (a + 1) * 128)
         cell = cell_in[0:1, part].astype(F32)
@@ -150,6 +177,25 @@
         for sweep in range(3):
             ref[sweep * groups] = jnp.zeros(ref.shape[1:], F32)
 
+    def cut(load, c):
+        start = c * chunk - margin
+        if start < 0:
+            return jnp.concatenate([load(LON + start, LON), load(0, LANES + start)], axis=1)
+        if start + LANES > LON:
+            return jnp.concatenate([load(start, LON), load(0, start + LANES - LON)], axis=1)
+        return load(start, start + LANES)
+
+    for fetch in fetches[4:7]:
+        fetch.wait()
+    for r in range(LAT):
+        for c in range(3):
+            q = (r * 3 + c) * 2
+            coef72[q // 8, q % 8 : q % 8 + 2, :] = coef3[c, :, r, :]
+    for c in range(windows):
+        for q in range(LAT * 6 // 8):
+            coef_in[c, q] = cut(lambda a, b, q=q: coef72[q, :, a:b], c)
+    craw[m] = coef_in[m]
+
     pl.semaphore_wait(barrier, tiles - 1 + 3 * (windows - 1))
 
     def remote(source, target, send, recv, where):
@@ -172,8 +218,6 @@
 
     lax.fori_loop(1, tiles, obs_start, 0)
 
-    coef_own = pltpu.make_async_copy(coef_in.at[m], craw.at[m], c_s.at[0])
-    coef_own.start()
 
     def coef_copy(d):
         peer = lax.rem(m + d, windows)
@@ -187,23 +231,19 @@
         coef_copy(d).start()
         return token
 
-    lax.fori_loop(1, windows, coef_start, 0)
-
-    raw_copy.wait()
+    @pl.when(m >= windows - GROUP)
+    def _():
+        lax.fori_loop(1, windows, coef_start, 0)
+
+    fetches[7].wait()
     for c in range(windows):
-        start = c * chunk - margin
         for r in range(LAT):
-            if start < 0:
-                piece = jnp.concatenate(
-                    [bvraw[:, r, LON + start : LON], bvraw[:, r, 0 : LANES + start]], axis=1
-                )
-            elif start + LANES > LON:
-                piece = jnp.concatenate(
-                    [bvraw[:, r, start:LON], bvraw[:, r, 0 : start + LANES - LON]], axis=1
-                )
-            else:
-                piece = bvraw[:, r, start : start + LANES]
-            bvpack[c, r] = piece
+            bvpack[c, r] = cut(lambda a, b, r=r: bvraw[:, r, a:b], c)
+
+    @pl.when(m < windows - GROUP)
+    def _():
+        lax.fori_loop(1, windows, coef_start, 0)
+
     bvr[m] = bvpack[m]
 
     obs1[t] = obs0[t]
@@ -240,16 +280,10 @@
 
     lax.fori_loop(1, windows, bv_start, 0)
 
-    def from_peer(ref, sem, k, own):
+    def from_peer(ref, sem, k):
         @pl.when(k != m)
         def _():
             remote(ref.at[k], ref.at[k], sem.at[k], sem.at[k], (k, t)).wait_recv()
-
-        if own is not None:
-
-            @pl.when(k == m)
-            def _():
-                own.wait()
 
     whole = LAT * 6 // 8
     edge_tiles = HALO * 6 // 8
@@ -270,13 +304,12 @@
             (m, up),
         )
 
-    def coef_forward(i, token):
+    def coef_forward(i):
         for j in range(GROUP - 1, -1, -1):
             k = windows - GROUP - GROUP * i + j
-            from_peer(craw, c_r, k, coef_own)
+            from_peer(craw, c_r, k)
             coef_low(k, j).start()
             coef_high(k, j).start()
-        return token
 
     even = lax.rem(lax.broadcasted_iota(jnp.int32, (FIELDS, LANES), 0), 2) == 0
 
@@ -471,7 +504,7 @@
                 send_carry(i, e + 1)
             done(k)
 
-    lax.fori_loop(0, groups, coef_forward, 0)
+    coef_forward(0)
 
     def prepare(i):
         for j in range(GROUP - 1, -1, -1):
@@ -492,36 +525,39 @@
                     ).wait_recv()
                 make_hot(k, n)
             scatter(0, k, j, lambda n, k=k: obsall[k, n, 2] * (0.0 - obsall[k, n, 1]))
+
+    def expand_group(i):
         for j in range(GROUP - 1, -1, -1):
             expand(windows - GROUP - GROUP * i + j, j)
 
     prepare(0)
+    for i in range(1, groups):
+        coef_forward(i)
+    expand_group(0)
 
     def increments(i):
         for j in range(GROUP):
             k = windows - GROUP - GROUP * i + j
-            from_peer(bvr, bv_r, k, None)
+            from_peer(bvr, bv_r, k)
             inc[k] = -0.5 * (bvr[k] * inc[k])
             inc_low(k, j).start()
             inc_high(k, j).start()
 
     def first(i, token):
+        def done(k):
+            inc[k] = work[0, HALO : HALO + LAT]
+
+        adjoint_group(0, i, done)
+
         @pl.when(i < groups - 1)
         def _():
             prepare(i + 1)
-
-        @pl.when(i > 0)
-        def _():
-            increments(i - 1)
-
-        def done(k):
-            inc[k] = work[0, HALO : HALO + LAT]
-
-        adjoint_group(0, i, done)
+            expand_group(i + 1)
+
+        increments(i)
         return token
 
     lax.fori_loop(0, groups, first, 0)
-    increments(groups - 1)
 
     def observe(i):
         for j in range(GROUP):
@@ -602,23 +638,31 @@
 
 
     def third(i, token):
+        def done(k):
+            old = inc[k]
+            states[k] = old - 0.5 * (old + bvr[k] * work[0, HALO : HALO + LAT])
+            for r in range(0, LAT, 2):
+                pair = []
+                for e in range(2):
+                    row = pltpu.roll(states[k, r + e], LANES - margin, 1)
+                    final[k, r + e] = row[:, :128]
+                    pair.append(row[:, 128:])
+                final[k, LAT + r // 2] = jnp.where(lane < 64, pair[0], pltpu.roll(pair[1], 64, 1))
+
+            @pl.when(k != m)
+            def _():
+                out_copy(k).start()
+
+            @pl.when(k == m)
+            def _():
+                result[k] = final[k]
+
+        adjoint_group(1, i, done)
+
         @pl.when(i < groups - 1)
         def _():
             regrid(i + 1)
 
-        def done(k):
-            old = inc[k]
-            final[k] = old - 0.5 * (old + bvr[k] * work[0, HALO : HALO + LAT])
-
-            @pl.when(k != m)
-            def _():
-                out_copy(k).start()
-
-            @pl.when(k == m)
-            def _():
-                result[k] = final[k]
-
-        adjoint_group(1, i, done)
         return token
 
     lax.fori_loop(0, groups, third, 0)
@@ -669,10 +713,14 @@
         return token
 
     lax.fori_loop(0, windows, finish_windows, 0)
+    tail = chunk - 128
     for r in range(LAT):
-        out_ref[:, r, :] = jnp.concatenate(
-            [result[c, r, :, margin : margin + chunk] for c in range(windows)], axis=1
-        )
+        first_lane = 64 * (r % 2)
+        pieces = []
+        for c in range(windows):
+            pieces.append(result[c, r])
+            pieces.append(result[c, LAT + r // 2, :, first_lane : first_lane + tail])
+        out_ref[:, r, :] = jnp.concatenate(pieces, axis=1)
 
 
 def per_device(
@@ -681,32 +729,22 @@
     windows = lax.axis_size("tm")
     tiles = lax.axis_size("tile")
     groups = windows // GROUP
-    chunk = LON // windows
-    margin = (LANES - chunk) // 2
     slots = tiles * CAP
-
-    def chunks(array):
-        wide = jnp.concatenate([array[..., -margin:], array, array[..., :margin]], axis=-1)
-        return jnp.stack([wide[..., c * chunk : c * chunk + LANES] for c in range(windows)])
-
-    coefs = jnp.stack([advect_east[0], advect_north[0], diffusion[0]])
-    coefs = chunks(coefs.transpose(2, 0, 1, 3).reshape(LAT * 6, LON))
-    coefs = coefs.reshape(windows, LAT * 6 // 8, 8, LANES)
     field = (FIELDS, LANES)
     dma = pltpu.SemaphoreType.DMA
     out = pl.pallas_call(
         functools.partial(kernel, windows, tiles),
         out_shape=jax.ShapeDtypeStruct((FIELDS, LAT, LON), F32),
-        in_specs=[
-            pl.BlockSpec(memory_space=pl.ANY),
-            pl.BlockSpec(memory_space=pl.ANY),
-            pl.BlockSpec(memory_space=pltpu.VMEM),
-            pl.BlockSpec(memory_space=pltpu.VMEM),
-            pl.BlockSpec(memory_space=pltpu.VMEM),
-            pl.BlockSpec(memory_space=pltpu.SMEM),
-        ],
+        in_specs=[pl.BlockSpec(memory_space=pl.ANY)] * 8,
         out_specs=pl.BlockSpec(memory_space=pltpu.VMEM),
         scratch_shapes=[
+            pltpu.VMEM((3, 2, LAT, LON), F32),
+            pltpu.VMEM((LAT * 6 // 8, 8, LON), F32),
+            pltpu.VMEM((windows, LAT * 6 // 8, 8, LANES), F32),
+            pltpu.VMEM((1, slots), jnp.int32),
+            pltpu.VMEM((1, slots), F32),
+            pltpu.VMEM((1, slots), F32),
+            pltpu.SMEM((1, tiles), jnp.int32),
             pltpu.VMEM((tiles, 4, 128), F32),
             pltpu.VMEM((tiles, 4, 128), F32),
             pltpu.VMEM((windows, 3, 3, 1, slots), F32),
@@ -723,11 +761,11 @@
             pltpu.VMEM((windows, HALO) + field, F32),
             pltpu.VMEM((windows, HALO) + field, F32),
             pltpu.VMEM((windows, LAT) + field, F32),
-            pltpu.VMEM((windows, LAT) + field, F32),
+            pltpu.VMEM((windows, LAT * 3 // 2, FIELDS, 128), F32),
             pltpu.VMEM((3 * groups, LAT) + field, F32),
             pltpu.VMEM((3 * groups, HALO) + field, F32),
             pltpu.VMEM((3 * groups, HALO) + field, F32),
-            pltpu.VMEM((windows, LAT) + field, F32),
+            pltpu.VMEM((windows, LAT * 3 // 2, FIELDS, 128), F32),
             pltpu.VMEM((2, ROWS) + field, F32),
             pltpu.VMEM((windows, 1, slots), F32),
             pltpu.VMEM((8, windows, 1, slots), F32),
@@ -739,7 +777,7 @@
             dma((windows,)),
             dma((2, windows)),
             dma((2, windows)),
-            dma,
+            dma((8,)),
             dma((windows,)),
             dma((windows,)),
             dma((2, windows)),
@@ -755,7 +793,9 @@
             collective_id=0, has_side_effects=True, vmem_limit_bytes=48 * 1024 * 1024
         ),
     )(
-        coefs,
+        advect_east[0],
+        advect_north[0],
+        diffusion[0],
         background_var.reshape(FIELDS, LAT, LON),
         obs_cell.reshape(1, slots),
         obs_value.reshape(1, slots),

time: 86.3 us -> 80.6 us (0.934)
  Pallas kernels: 81.1 us -> 76.2 us
  other arithmetic: 1.45 us -> 0 us
    pallas_call x1, Pallas kernels: 81.1 us -> 76.2 us  [per_device(): pl.pallas_call(functools.partial(kernel, windows, tiles), out_shape=jax.S...]
    transpose x1 -> x0, other arithmetic: 1.26 us -> none  [per_device(): coefs = chunks(coefs.transpose(2, 0, 1, 3).reshape(LAT * 6, LON))]
    squeeze x0 -> x1, local copies, waits for them, and re-layouts: none -> 1.04 us  [per_device(): diffusion[0]]
    unnamed x17 -> x12, local copies, waits for them, and re-layouts: 1.89 us -> 1.8 us
where the time goes in v3:
time: 80.6 us; the launch traced here: 80.4 us
  Pallas kernels  76.2 us (95%)
  local copies, waits for them, and re-layouts  4.11 us (5%)
    pallas_call x1, Pallas kernels, per_device(): pl.pallas_call(functools.partial(kernel, windows, tiles), out_shape=jax.S...  76.2 us
    unnamed x12, local copies, waits for them, and re-layouts  1.8 us

profile of v3, /device:TPU:1, one launch (start us, length us, event | category | flops | bytes accessed | tf_op | source)
XLA Modules:
  0.0 80.4 jit_solution(17978692568327142950)
XLA Ops:
  0.0 0.0 copy-start.4
  0.0 1.0 %copy.17 = f32[1,2,12,1440]{3,2,1,0:T(8,128)S(1)} copy(f32[1,2,12,1440]{3,1,2,0:T(2,128)} %param.8) | data formatting | bytes 276480 | tf_op args[0]
  1.0 1.0 %copy_bitcast_fusion = (f32[2,12,1440]{2,1,0:T(8,128)S(1)}, f32[2,12,1440]{2,1,0:T(8,128)S(1)}) fusion(f32[1,2,12,1440]{3,1,2,0:T(2,128)} %param.10, f32[1,2,12,1440]{3,1,2,0:T(2,128)} %param.9), kind=kLoop, calls=%fused_computation | loop fusion | bytes 552960 | tf_op jit(solution)/shard_map/squeeze | solution.py:798
  2.1 0.0 copy-done.4
  2.1 0.0 copy-start
  2.1 0.0 copy-start.1
  2.1 0.0 copy-start.2
  2.1 0.1 copy.12
  2.2 0.0 copy-start.3
  2.2 0.5 copy-done
  2.8 0.0 copy-done.1
  2.8 0.0 copy-done.2
  2.8 0.1 copy-done.3
  2.9 76.2 %shard_map.82 = f32[8,12,1440]{2,1,0:T(8,128)S(1)} custom-call(f32[2,12,1440]{2,1,0:T(8,128)S(1)} %bitcast.15, f32[2,12,1440]{2,1,0:T(8,128)S(1)} %get-tuple-element.6.north_hbm, f32[2,12,1440]{2,1,0:T(8,128)S(1)} %get-tuple-element.5.diff_hbm, f32[8,12,1440]{2,1,0:T(8,128)S(1)} %bitcast.14, s32[1,1024]{1,0:T(1,128)S(1)} %bitcast.16, ...), custom_call_target="tpu_custom_call" | custom-call | tf_op jit(solution)/shard_map/pallas_call | solution.py:735
  79.1 1.3 %copy.13 = f32[1,4,2,12,1440]{4,2,3,1,0:T(2,128)} copy(f32[1,4,2,12,1440]{4,3,2,1,0:T(8,128)S(1)} %bitcast.13) | data formatting | bytes 1105920 | tf_op jit(solution)/shard_map/reshape | solution.py:805
Async XLA Ops:
  0.0 2.1 %copy-start.4 = (f32[1,4,2,12,1440]{4,2,3,1,0:T(2,128)S(1)}, f32[1,4,2,12,1440]{4,2,3,1,0:T(2,128)}, u32[]{:S(2)}) copy-start(f32[1,4,2,12,1440]{4,2,3,1,0:T(2,128)} %param.11) | copy-start | bytes 1658884
  2.1 0.7 copy-start
  2.1 0.7 copy-start.1
  2.1 0.7 copy-start.2
  2.2 0.7 copy-start.3

commit v4 on v3

--- a/solution.py
+++ b/solution.py
@@ -55,6 +55,7 @@
     craws,
     der,
     bvraw,
+    bv8,
     bvpack,
     bvr,
     hot,
@@ -67,7 +68,6 @@
     carry,
     carryn,
     carrys,
-    result,
     work,
     innov,
     arrived,
@@ -190,7 +190,7 @@
     for r in range(LAT):
         for c in range(3):
             q = (r * 3 + c) * 2
-            coef72[q // 8, q % 8 : q % 8 + 2, :] = coef3[c, :, r, :]
+            coef72[q // 8, q % 8 : q % 8 + 2, :] = coef3[c, r]
     for c in range(windows):
         for q in range(LAT * 6 // 8):
             coef_in[c, q] = cut(lambda a, b, q=q: coef72[q, :, a:b], c)
@@ -236,9 +236,12 @@
         lax.fori_loop(1, windows, coef_start, 0)
 
     fetches[7].wait()
+    for r in range(LAT):
+        for v in range(FIELDS // 2):
+            bv8[r, 2 * v : 2 * v + 2, :] = bvraw[v, r]
     for c in range(windows):
         for r in range(LAT):
-            bvpack[c, r] = cut(lambda a, b, r=r: bvraw[:, r, a:b], c)
+            bvpack[c, r] = cut(lambda a, b, r=r: bv8[r, :, a:b], c)
 
     @pl.when(m < windows - GROUP)
     def _():
@@ -634,8 +637,11 @@
     regrid(0)
 
     def out_copy(k):
-        return remote(final.at[k], result.at[m], out_s.at[k], out_r.at[m], (k, t))
-
+        return remote(final.at[k], out_ref.at[m], out_s.at[k], out_r.at[m], (k, t))
+
+
+    def out_own(k):
+        return pltpu.make_async_copy(final.at[k], out_ref.at[m], out_r.at[k])
 
     def third(i, token):
         def done(k):
@@ -655,7 +661,7 @@
 
             @pl.when(k == m)
             def _():
-                result[k] = final[k]
+                out_own(k).start()
 
         adjoint_group(1, i, done)
 
@@ -707,20 +713,29 @@
     def finish_windows(k, token):
         @pl.when(k != m)
         def _():
-            remote(final.at[k], result.at[k], out_s.at[k], out_r.at[k], (k, t)).wait_recv()
+            remote(final.at[k], out_ref.at[k], out_s.at[k], out_r.at[k], (k, t)).wait_recv()
             out_copy(k).wait_send()
 
+        @pl.when(k == m)
+        def _():
+            out_own(k).wait()
+
         return token
 
     lax.fori_loop(0, windows, finish_windows, 0)
-    tail = chunk - 128
-    for r in range(LAT):
-        first_lane = 64 * (r % 2)
+
+
+def unpack(main_ref, tail_ref, out_ref):
+    windows = main_ref.shape[0]
+    tail = LON // windows - 128
+    for e in range(2):
         pieces = []
         for c in range(windows):
-            pieces.append(result[c, r])
-            pieces.append(result[c, LAT + r // 2, :, first_lane : first_lane + tail])
-        out_ref[:, r, :] = jnp.concatenate(pieces, axis=1)
+            pieces.append(main_ref[c, e])
+            pieces.append(tail_ref[c, 0, :, 64 * e : 64 * e + tail])
+        row = jnp.concatenate(pieces, axis=1)
+        for v in range(FIELDS // 2):
+            out_ref[v, e] = row[2 * v : 2 * v + 2, :]
 
 
 def per_device(
@@ -732,13 +747,13 @@
     slots = tiles * CAP
     field = (FIELDS, LANES)
     dma = pltpu.SemaphoreType.DMA
-    out = pl.pallas_call(
+    packed = pl.pallas_call(
         functools.partial(kernel, windows, tiles),
-        out_shape=jax.ShapeDtypeStruct((FIELDS, LAT, LON), F32),
-        in_specs=[pl.BlockSpec(memory_space=pl.ANY)] * 8,
-        out_specs=pl.BlockSpec(memory_space=pltpu.VMEM),
+        out_shape=jax.ShapeDtypeStruct((windows, LAT * 3 // 2, FIELDS, 128), F32),
+        in_specs=[pl.BlockSpec(memory_space=pltpu.HBM)] * 8,
+        out_specs=pl.BlockSpec(memory_space=pl.ANY),
         scratch_shapes=[
-            pltpu.VMEM((3, 2, LAT, LON), F32),
+            pltpu.VMEM((3, LAT, 2, LON), F32),
             pltpu.VMEM((LAT * 6 // 8, 8, LON), F32),
             pltpu.VMEM((windows, LAT * 6 // 8, 8, LANES), F32),
             pltpu.VMEM((1, slots), jnp.int32),
@@ -752,7 +767,8 @@
             pltpu.VMEM((windows, HALO * 6 // 8, 8, LANES), F32),
             pltpu.VMEM((windows, HALO * 6 // 8, 8, LANES), F32),
             pltpu.VMEM((windows, 5, ROWS) + field, F32),
-            pltpu.VMEM((FIELDS, LAT, LON), F32),
+            pltpu.VMEM((FIELDS // 2, LAT, 2, LON), F32),
+            pltpu.VMEM((LAT, FIELDS, LON), F32),
             pltpu.VMEM((windows, LAT) + field, F32),
             pltpu.VMEM((windows, LAT) + field, F32),
             pltpu.VMEM((windows, 3, LANES, slots), BF16),
@@ -765,7 +781,6 @@
             pltpu.VMEM((3 * groups, LAT) + field, F32),
             pltpu.VMEM((3 * groups, HALO) + field, F32),
             pltpu.VMEM((3 * groups, HALO) + field, F32),
-            pltpu.VMEM((windows, LAT * 3 // 2, FIELDS, 128), F32),
             pltpu.VMEM((2, ROWS) + field, F32),
             pltpu.VMEM((windows, 1, slots), F32),
             pltpu.VMEM((8, windows, 1, slots), F32),
@@ -790,19 +805,29 @@
             dma((windows,)),
         ],
         compiler_params=pltpu.CompilerParams(
-            collective_id=0, has_side_effects=True, vmem_limit_bytes=48 * 1024 * 1024
+            collective_id=0, has_side_effects=True, vmem_limit_bytes=65000000
         ),
     )(
-        advect_east[0],
-        advect_north[0],
-        diffusion[0],
-        background_var.reshape(FIELDS, LAT, LON),
+        advect_east[0].transpose(1, 0, 2),
+        advect_north[0].transpose(1, 0, 2),
+        diffusion[0].transpose(1, 0, 2),
+        background_var[0].transpose(0, 2, 1, 3),
         obs_cell.reshape(1, slots),
         obs_value.reshape(1, slots),
         obs_weight.reshape(1, slots),
         obs_count.reshape(1, tiles),
     )
-    return out.reshape(1, FIELDS // 2, 2, LAT, LON)
+    out = pl.pallas_call(
+        unpack,
+        out_shape=jax.ShapeDtypeStruct((FIELDS // 2, LAT, 2, LON), F32),
+        grid=(LAT // 2,),
+        in_specs=[
+            pl.BlockSpec((windows, 2, FIELDS, 128), lambda p: (0, p, 0, 0)),
+            pl.BlockSpec((windows, 1, FIELDS, 128), lambda p: (0, LAT + p, 0, 0)),
+        ],
+        out_specs=pl.BlockSpec((FIELDS // 2, 2, 2, LON), lambda p: (0, p, 0, 0)),
+    )(packed, packed)
+    return out.transpose(0, 2, 1, 3)[None]
 
 
 def solution(mesh):

time: 80.6 us -> 79.8 us (0.990)
  local copies, waits for them, and re-layouts: 4.11 us -> 0 us
  Pallas kernels: 76.2 us -> 79.4 us
    pallas_call x0 -> x1, Pallas kernels: none -> 4.21 us  [per_device(): pl.pallas_call(unpack, out_shape=jax.ShapeDtypeStruct((FIELDS // 2, LAT,...]
    unnamed x12 -> x0, local copies, waits for them, and re-layouts: 1.8 us -> none
    reshape x1 -> x0, local copies, waits for them, and re-layouts: 1.27 us -> none  [per_device(): return out.reshape(1, FIELDS // 2, 2, LAT, LON)]
    squeeze x1 -> x0, local copies, waits for them, and re-layouts: 1.04 us -> none  [per_device(): diffusion[0]]
    pallas_call x1, Pallas kernels: 76.2 us -> 75.2 us  [per_device(): pl.pallas_call(functools.partial(kernel, windows, tiles), out_shape=jax.S...]
where the time goes in v4:
time: 79.8 us; the launch traced here: 79.4 us
  Pallas kernels  79.4 us (99%)
    pallas_call x1, Pallas kernels, per_device(): pl.pallas_call(functools.partial(kernel, windows, tiles), out_shape=jax.S...  75.2 us
    pallas_call x1, Pallas kernels, per_device(): pl.pallas_call(unpack, out_shape=jax.ShapeDtypeStruct((FIELDS // 2, LAT,...  4.21 us

profile of v4, /device:TPU:1, one launch (start us, length us, event | category | flops | bytes accessed | tf_op | source)
XLA Modules:
  0.0 79.4 jit_solution(6940003447396164131)
XLA Ops:
  0.0 75.2 %shard_map.82.main_ref.tail_ref = f32[8,18,8,128]{3,2,1,0:T(8,128)} custom-call(f32[12,2,1440]{2,1,0:T(2,128)} %bitcast.20, f32[12,2,1440]{2,1,0:T(2,128)} %bitcast.21, f32[12,2,1440]{2,1,0:T(2,128)} %bitcast.22, f32[4,12,2,1440]{3,2,1,0:T(2,128)} %bitcast.19, s32[1,1024]{1,0:T(1,128)} %bitcast.23, f32[1,1024]{1,0:T(1,128)} %bitcast.24, f32[1,1024]{1,0:T(1,128)} %bitcast.25, ...), custom_call_target="tpu_custom_call" | custom-call | tf_op jit(solution)/shard_map/pallas_call | solution.py:750
  75.2 4.2 %shard_map.83 = f32[4,12,2,1440]{3,2,1,0:T(2,128)} custom-call(f32[8,18,8,128]{3,2,1,0:T(8,128)} %shard_map.82.main_ref.tail_ref, f32[8,18,8,128]{3,2,1,0:T(8,128)} %shard_map.82.main_ref.tail_ref), custom_call_target="tpu_custom_call" | custom-call | tf_op jit(solution)/shard_map/pallas_call | solution.py:820
